TPU v7x, 32 devices: a whole 2x2x4 slice. The times are simulated.
32 devices in a mesh: row: 8 (over z, y), col: 4 (over x, core).
Axes of the slice: x: 2, y: 2, z: 4, core: 2. Of those that a mesh axis runs over, the one named last changes fastest.
Arguments:
- trailing: bfloat16 [12288, 12288], P('row', 'col'), may hold values from -6 to 6
- rows_a: int32 [8, 12], replicated, may hold values from 0 to 11, as said below
- counts_a: int32 [8], replicated, may hold values from 1 to 12, as said below
- factor_a: bfloat16 [12288, 512], P('row'), may hold values from -0.0546875 to 0.0546875
- rows_b: int32 [8, 12], replicated, may hold values from 0 to 11, as said below
- counts_b: int32 [8], replicated, may hold values from 1 to 12, as said below
- factor_b: bfloat16 [12288, 512], P('row'), may hold values from -0.0546875 to 0.0546875
- factor_top: bfloat16 [512, 512], replicated, may hold values from -0.25 to 0.25
- base_a: float32 [512, 512], P('col'), may hold values from -3 to 3
- base_b: float32 [512, 512], P('col'), may hold values from -3 to 3
Outputs:
- column_a: bfloat16 [12288, 512], P('row')
- diag_a: float32 [512, 512], P('col')
- column_b: bfloat16 [12288, 512], P('row')
- top_b: bfloat16 [512, 512], P('col')
- diag_b: float32 [512, 512], P('col')
Inputs may be any that keep to these rules, and one draw needn't show every extreme that they name: `rows_a`: the first counts_a[r] entries of row r are distinct; the rest of the row is padding. `counts_a`: some owner uses all 12 slots in every draw. `rows_b`: the first counts_b[r] entries of row r are distinct and lie among the first counts_a[r] entries of row r of rows_a; the rest is padding. counts_b[r] <= counts_a[r]; some owner uses all 12 slots in every draw.
All inputs are finite; a program needn't handle non-finite values.
Results may differ from a plain program's by a relative error of at most 0.007.
Values may be sent and summed in bfloat16 or wider, within the bound.
A program may use at most 128 MiB of HBM per device.

v0:
```python
import jax
import jax.numpy as jnp
from jax import lax
from jax.sharding import PartitionSpec as P


def contract_rows(former, latter):
    return lax.dot_general(
        former, latter, (((0,), (0,)), ((), ())), preferred_element_type=jnp.float32
    )


def on_device(
    trailing, rows_a, counts_a, factor_a, rows_b, counts_b, factor_b, factor_top, base_a, base_b
):
    row_count = lax.axis_size("row")
    col_count = lax.axis_size("col")
    fanout = row_count // col_count
    row_index = lax.axis_index("row")
    col_index = lax.axis_index("col")
    slots = rows_a.shape[1]
    total_rows, width = factor_a.shape
    block = total_rows // slots
    row_blocks = trailing.shape[0] // block
    part_width = width // col_count
    width_start = col_index * part_width
    slot_ids = jnp.arange(slots, dtype=jnp.int32)

    def own(table):
        return lax.dynamic_index_in_dim(table, row_index, 0, keepdims=False)

    live_a = slot_ids < own(counts_a)
    live_b = slot_ids < own(counts_b)
    own_a, own_b = own(rows_a), own(rows_b)
    blocks = jnp.arange(row_blocks, dtype=jnp.int32)
    gate_a = jnp.any((own_a[None, :] == blocks[:, None]) & live_a[None, :], axis=1)
    gate_b = jnp.any((own_b[None, :] == blocks[:, None]) & live_b[None, :], axis=1)

    pieces = jnp.stack([factor_a, factor_b]).reshape(
        2, row_count, total_rows // row_count, width
    )
    arrived = []
    for shift in range(row_count):
        piece = lax.dynamic_index_in_dim(
            pieces, (row_index + shift) % row_count, 1, keepdims=False
        )
        if shift:
            pairs = [
                (
                    owner * col_count + owner % col_count,
                    (owner + shift) % row_count * col_count + owner % col_count,
                )
                for owner in range(row_count)
            ]
            piece = lax.ppermute(piece, ("row", "col"), pairs)
        arrived.append(piece)
    arrived = jnp.stack(arrived)
    mine = jnp.stack(
        [
            lax.dynamic_index_in_dim(
                arrived,
                (row_index - col_index - part * col_count) % row_count,
                0,
                keepdims=False,
            )
            for part in range(fanout)
        ],
        axis=1,
    )
    held = lax.all_gather(mine, "row", axis=2, tiled=True)
    owners = col_index + jnp.arange(fanout, dtype=jnp.int32) * col_count

    def partial_product(node, rows, counts):
        own_rows = jnp.take(rows, owners, axis=0)
        live = slot_ids[None, :] < jnp.take(counts, owners, axis=0)[:, None]
        match = (own_rows[None, :, :] == blocks[:, None, None]) & live[None, :, :]
        filled = jnp.any(match, axis=2).reshape(-1)
        source = jnp.argmax(match, axis=2).astype(jnp.int32)
        source = (source + jnp.arange(fanout, dtype=jnp.int32) * slots).reshape(-1)
        picked = jnp.take(held[node].reshape(fanout * slots, block, width), source, axis=0)
        spread = jnp.where(filled[:, None, None], picked, 0).reshape(-1, width)
        return jnp.dot(trailing, spread, preferred_element_type=jnp.float32).astype(
            jnp.bfloat16
        )

    part = jnp.stack(
        [partial_product(0, rows_a, counts_a), partial_product(1, rows_b, counts_b)]
    )
    reduced = lax.psum_scatter(part, "col", scatter_dimension=2, tiled=True).astype(jnp.float32)

    def gated(value, gate):
        return jnp.where(
            gate[:, None, None], value.reshape(row_blocks, block, -1), 0
        ).reshape(row_blocks * block, -1)

    def by_slot(value, own_rows, live):
        picked = jnp.take(value.reshape(row_blocks, block, -1), own_rows, axis=0)
        return jnp.where(live[:, None, None], picked, 0).reshape(total_rows, -1)

    col_a = gated(-reduced[0], gate_a).astype(jnp.bfloat16)
    whole_a = lax.all_gather(col_a, "col", axis=1, tiled=True)
    column_a = by_slot(whole_a, own_a, live_a)
    top_part = lax.dynamic_slice_in_dim(factor_top, width_start, part_width, 1)
    cross = jnp.dot(whole_a, top_part, preferred_element_type=jnp.float32)
    col_b = gated(-(reduced[1] + cross), gate_b).astype(jnp.bfloat16)
    column_b = by_slot(
        lax.all_gather(col_b, "col", axis=1, tiled=True), own_b, live_b
    )
    sums = lax.psum(
        (
            contract_rows(by_slot(col_a, own_a, live_a), factor_a),
            contract_rows(by_slot(col_a, own_b, live_b), factor_b),
            contract_rows(by_slot(col_b, own_b, live_b), factor_b),
        ),
        "row",
    )
    diag_a = base_a - sums[0]
    top_b = (
        -(
            sums[1]
            + jnp.dot(diag_a, factor_top.astype(jnp.float32), precision=lax.Precision.HIGHEST)
        )
    ).astype(jnp.bfloat16)
    top_whole = lax.all_gather(top_b, "col", axis=0, tiled=True)
    top_cols = lax.dynamic_slice_in_dim(top_whole, width_start, part_width, 1)
    diag_b = base_b - sums[2] - contract_rows(top_cols, factor_top)
    return (column_a, diag_a, column_b, top_b, diag_b)


def solution(mesh):
    in_specs = (
        P("row", "col"),
        P(),
        P(),
        P("row", None),
        P(),
        P(),
        P("row", None),
        P(),
        P("col", None),
        P("col", None),
    )
    out_specs = (P("row", None), P("col", None), P("row", None), P("col", None), P("col", None))
    return jax.shard_map(
        on_device, mesh=mesh, in_specs=in_specs, out_specs=out_specs, check_vma=False
    )
```

profile of v0, /device:TPU:1, one launch (start us, length us, event | category | flops | bytes accessed | tf_op | source)
XLA Modules:
  0.0 358.8 jit_solution(10162166294966140)
XLA Ops:
  7.3 2.9 fusion.22
  10.2 1.4 collective-permute-start
  11.7 1.4 collective-permute-start.1
  13.1 1.3 collective-permute-start.2
  14.4 1.4 collective-permute-start.3
  15.8 1.4 collective-permute-start.4
  17.2 1.7 bitcast_dynamic-update-slice_fusion.7
  18.9 1.1 fusion.16
  20.0 0.7 collective-permute-start.5
  20.9 1.0 bitcast_dynamic-update-slice_fusion.6
  21.9 1.3 collective-permute-start.6
  23.2 1.0 bitcast_dynamic-update-slice_fusion.5
  24.3 2.8 collective-permute-done.2
  27.0 1.0 bitcast_dynamic-update-slice_fusion.4
  28.1 1.0 bitcast_dynamic-update-slice_fusion.3
  29.1 1.0 bitcast_dynamic-update-slice_fusion.2
  30.2 8.0 %collective-permute-done.6 = bf16[2,192,512]{2,1,0:T(8,128)(2,1)S(1)} collective-permute-done((bf16[2,192,512]{2,1,0:T(8,128)(2,1)S(1)}, bf16[2,192,512]{2,1,0:T(8,128)(2,1)S(1)}, u32[]{:S(2)}, u32[]{:S(2)}) %collective-permute-start.6) | collective-permute-done | bytes 393248 | tf_op jit(solution)/shard_map/ppermute | solution.py:55
  38.3 0.9 pad_maximum_fusion.1
  39.4 0.6 gather_fusion
  39.9 0.6 gather_fusion.3
  40.5 0.6 gather_fusion.1
  41.1 0.6 gather_fusion.4
  42.0 1.1 iota_reduce_fusion.1
  43.1 1.1 iota_reduce_fusion
  45.1 98.8 %all-gather.4.cloned.1.call-done = bf16[2,2,1536,512]{3,2,0,1:T(8,128)(2,1)} async-done(((bf16[2,2,192,512]{3,2,0,1:T(8,128)(2,1)}), bf16[2,2,1536,512]{3,2,0,1:T(8,128)(2,1)}) %all-gather.4.cloned.1.call-update) | async-done | bytes 6291472 | tf_op jit(solution)/shard_map/all_gather | solution.py:70
  143.9 5.9 %fusion.37 = (bf16[1,2,1536,512]{3,2,0,1:T(8,128)(2,1)}, bf16[1,2,1536,512]{3,2,0,1:T(8,128)(2,1)}) fusion(bf16[2,2,1536,512]{3,2,0,1:T(8,128)(2,1)} %all-gather.4.cloned.1.call-done), kind=kLoop, calls=%fused_computation.126 | loop fusion | bytes 12582912 | tf_op jit(solution)/shard_map/slice | solution.py:80
  149.8 4.4 %gather_fusion.2 = bf16[24,128,512]{2,1,0:T(8,128)(2,1)} fusion(bf16[24,128,512]{2,1,0:T(8,128)(2,1)} %bitcast.98, s32[1024]{0:T(1024)S(1)} %pad_clamp_fusion.3), kind=kCustom, calls=%fused_computation.2.clone | custom fusion | bytes 6291552 | tf_op jit(solution)/shard_map/jit(_take)/gather | solution.py:80
  154.2 2.3 select_select_fusion.1
  156.5 9.0 %fusion = bf16[1,1536,512]{1,2,0:T(8,128)(2,1)} fusion(bf16[3072,512]{1,0:T(8,128)(2,1)S(1)} %bitcast.101, bf16[1536,3072]{1,0:T(8,128)(2,1)} %param.20), kind=kOutput, calls=%fused_computation.32 | convolution fusion | flops 4832624640 | bytes 14155776 | tf_op jit(solution)/shard_map/dot_general | solution.py:82
  165.5 4.4 %gather_fusion.5 = bf16[24,128,512]{2,1,0:T(8,128)(2,1)} fusion(bf16[24,128,512]{2,1,0:T(8,128)(2,1)} %bitcast.97, s32[1024]{0:T(1024)S(1)} %pad_clamp_fusion.2), kind=kCustom, calls=%fused_computation.7.clone | custom fusion | bytes 6291552 | tf_op jit(solution)/shard_map/jit(_take)/gather | solution.py:80
  169.9 2.3 select_select_fusion
  172.2 8.0 %fusion.1 = bf16[1,1536,512]{1,2,0:T(8,128)(2,1)S(1)} fusion(bf16[3072,512]{1,0:T(8,128)(2,1)S(1)} %bitcast.102, bf16[1536,3072]{1,0:T(8,128)(2,1)} %param.20), kind=kOutput, calls=%fused_computation.33 | convolution fusion | flops 4832624640 | bytes 14155776 | tf_op jit(solution)/shard_map/dot_general | solution.py:82
  180.2 1.9 pad_maximum_fusion
  182.2 0.6 dynamic_slice.52
  182.8 0.6 dynamic_slice.64
  183.3 0.6 iota_compare_fusion.5
  184.2 35.3 %reduce-scatter.2.cloned.1.call-done = bf16[2,1536,128]{1,2,0:T(8,128)(2,1)} async-done(((bf16[2,1536,512]{1,2,0:T(8,128)(2,1)}), bf16[2,1536,128]{1,2,0:T(8,128)(2,1)}) %reduce-scatter.2.cloned.1.call-update) | async-done | bytes 786448 | tf_op jit(solution)/shard_map/reduce_scatter | solution.py:89
  219.5 1.3 convert_element_type.45
  220.8 1.1 copy-done.4
  221.9 0.8 fusion.7
  223.0 0.7 iota_compare_fusion.4
  223.9 1.2 slice_negate_fusion
  225.5 0.6 gather_fusion.9
  226.1 0.6 gather_fusion.7
  226.9 2.5 fusion.38
  229.4 13.7 %all-gather.6.cloned.1.call-done = bf16[1536,512]{0,1:T(8,128)(2,1)} async-done(((bf16[1536,128]{0,1:T(8,128)(2,1)}), bf16[1536,512]{0,1:T(8,128)(2,1)}) %all-gather.6.cloned.1.call-update) | async-done | bytes 1572880 | tf_op jit(solution)/shard_map/all_gather | solution.py:101
  243.1 2.0 fusion.4
  245.4 1.4 gather_fusion.10
  246.8 1.2 select_select_fusion.4
  248.0 1.1 fusion.39
  249.1 1.1 fusion.40
  250.2 0.5 all-gather.8.cloned.1.call-update
  250.8 2.6 copy.27
  253.4 2.1 gather_fusion.6
  255.5 1.4 select_select_fusion.3
  256.9 67.4 %all-reduce.3.cloned.1.call-done = (f32[128,512]{1,0:T(8,128)}, f32[128,512]{1,0:T(8,128)}, f32[128,512]{1,0:T(8,128)}) async-done(((f32[128,512]{1,0:T(8,128)}, f32[128,512]{1,0:T(8,128)}, f32[128,512]{1,0:T(8,128)}), (f32[128,512]{1,0:T(8,128)}, f32[128,512]{1,0:T(8,128)}, f32[128,512]{1,0:T(8,128)})) %all-reduce.3.cloned.1.call-update) | async-done | bytes 786448 | tf_op jit(solution)/shard_map/psum | solution.py:109
  324.3 1.0 sub.18
  325.3 1.4 fusion.6
  326.8 9.0 %all_gather.15 = bf16[512,512]{1,0:T(8,128)(2,1)S(1)} all-gather(bf16[128,512]{1,0:T(8,128)(2,1)S(1)} %fusion.6), channel_id=1, replica_groups=mesh['row'=8,'col'=4] {'col'}, dimensions={0}, use_global_device_ids=true | all-gather | bytes 655360 | tf_op jit(solution)/shard_map/all_gather | solution.py:124
  335.7 1.9 convolution_subtract_fusion
  337.6 8.6 %all-gather.8.cloned.1.call-done = bf16[1536,512]{0,1:T(8,128)(2,1)} async-done(((bf16[1536,128]{0,1:T(8,128)(2,1)}), bf16[1536,512]{0,1:T(8,128)(2,1)}) %all-gather.8.cloned.1.call-update) | async-done | bytes 1572880 | tf_op jit(solution)/shard_map/all_gather | solution.py:107
  346.2 2.6 copy.30
  348.8 2.1 gather_fusion.8
  350.9 1.4 select_select_fusion.2
  (76 shorter events, 3.1 us)
Async XLA Ops:
  7.2 236.0 %copy-start = (bf16[512,512]{1,0:T(8,128)(2,1)S(1)}, bf16[512,512]{1,0:T(8,128)(2,1)}, u32[]{:S(2)}) copy-start(bf16[512,512]{1,0:T(8,128)(2,1)} %param.27) | copy-start | bytes 1572868
  7.2 10.0 %copy-start.3 = (bf16[1536,512]{1,0:T(8,128)(2,1)S(1)}, bf16[1536,512]{1,0:T(8,128)(2,1)}, u32[]{:S(2)}) copy-start(bf16[1536,512]{1,0:T(8,128)(2,1)} %param.26) | copy-start | bytes 4718596
  7.2 136.7 %all-gather.4.cloned.1.call-start = ((), (), s32[]{:S(2)}) async-start(), calls=%async_computation.1 | async-start | bytes 7077888 | tf_op jit(solution)/shard_map/all_gather | solution.py:70
  10.2 9.8 %collective-permute-start = (bf16[2,192,512]{2,1,0:T(8,128)(2,1)}, bf16[2,192,512]{2,1,0:T(8,128)(2,1)}, u32[]{:S(2)}, u32[]{:S(2)}) collective-permute-start(bf16[2,192,512]{2,1,0:T(8,128)(2,1)} %get-tuple-element.26), channel_id=1, source_target_pairs={{0,4},{5,9},{10,14},{15,19},{16,20},{21,25},{26,30},{31,3}} | collective-permute-start | bytes 1179656 | tf_op jit(solution)/shard_map/ppermute | solution.py:55
  11.7 10.3 %collective-permute-start.1 = (bf16[2,192,512]{2,1,0:T(8,128)(2,1)}, bf16[2,192,512]{2,1,0:T(8,128)(2,1)}, u32[]{:S(2)}, u32[]{:S(2)}) collective-permute-start(bf16[2,192,512]{2,1,0:T(8,128)(2,1)} %get-tuple-element.27), channel_id=1, source_target_pairs={{0,8},{5,13},{10,18},{15,23},{16,24},{21,29},{26,2},{31,7}} | collective-permute-start | bytes 1179656 | tf_op jit(solution)/shard_map/ppermute | solution.py:55
  13.1 13.9 %collective-permute-start.2 = (bf16[2,192,512]{2,1,0:T(8,128)(2,1)}, bf16[2,192,512]{2,1,0:T(8,128)(2,1)}, u32[]{:S(2)}, u32[]{:S(2)}) collective-permute-start(bf16[2,192,512]{2,1,0:T(8,128)(2,1)} %get-tuple-element.28), channel_id=1, source_target_pairs={{0,12},{5,17},{10,22},{15,27},{16,28},{21,1},{26,6},{31,11}} | collective-permute-start | bytes 1179656 | tf_op jit(solution)/shard_map/ppermute | solution.py:55
  14.4 13.7 %collective-permute-start.3 = (bf16[2,192,512]{2,1,0:T(8,128)(2,1)S(1)}, bf16[2,192,512]{2,1,0:T(8,128)(2,1)}, u32[]{:S(2)}, u32[]{:S(2)}) collective-permute-start(bf16[2,192,512]{2,1,0:T(8,128)(2,1)S(1)} %get-tuple-element.29), channel_id=1, source_target_pairs={{0,16},{5,21},{10,26},{15,31},{16,0},{21,5},{26,10},{31,15}} | collective-permute-start | bytes 1179656 | tf_op jit(solution)/shard_map/ppermute | solution.py:55
  15.8 13.3 %collective-permute-start.4 = (bf16[2,192,512]{2,1,0:T(8,128)(2,1)S(1)}, bf16[2,192,512]{2,1,0:T(8,128)(2,1)}, u32[]{:S(2)}, u32[]{:S(2)}) collective-permute-start(bf16[2,192,512]{2,1,0:T(8,128)(2,1)S(1)} %get-tuple-element.30), channel_id=1, source_target_pairs={{0,20},{5,25},{10,30},{15,3},{16,4},{21,9},{26,14},{31,19}} | collective-permute-start | bytes 1179656 | tf_op jit(solution)/shard_map/ppermute | solution.py:55
  18.9 2.0 copy-start.9
  20.0 10.1 %collective-permute-start.5 = (bf16[2,192,512]{2,1,0:T(8,128)(2,1)S(1)}, bf16[2,192,512]{2,1,0:T(8,128)(2,1)S(1)}, u32[]{:S(2)}, u32[]{:S(2)}) collective-permute-start(bf16[2,192,512]{2,1,0:T(8,128)(2,1)S(1)} %fusion.16), channel_id=1, source_target_pairs={{0,24},{5,29},{10,2},{15,7},{16,8},{21,13},{26,18},{31,23}} | collective-permute-start | bytes 1179656 | tf_op jit(solution)/shard_map/ppermute | solution.py:55
  21.9 16.3 %collective-permute-start.6 = (bf16[2,192,512]{2,1,0:T(8,128)(2,1)S(1)}, bf16[2,192,512]{2,1,0:T(8,128)(2,1)S(1)}, u32[]{:S(2)}, u32[]{:S(2)}) collective-permute-start(bf16[2,192,512]{2,1,0:T(8,128)(2,1)S(1)} %get-tuple-element.25), channel_id=1, source_target_pairs={{0,28},{5,1},{10,6},{15,11},{16,12},{21,17},{26,22},{31,27}} | collective-permute-start | bytes 1179656 | tf_op jit(solution)/shard_map/ppermute | solution.py:55
  29.1 10.3 %copy-start.12 = (s32[8,12]{1,0:T(8,128)S(1)}, s32[8,12]{1,0:T(8,128)}, u32[]{:S(2)}) copy-start(s32[8,12]{1,0:T(8,128)} %param.21) | copy-start | bytes 1156
  29.1 10.8 %copy-start.13 = (s32[8,12]{1,0:T(8,128)S(1)}, s32[8,12]{1,0:T(8,128)}, u32[]{:S(2)}) copy-start(s32[8,12]{1,0:T(8,128)} %param.24) | copy-start | bytes 1156
  29.1 11.4 %copy-start.1 = (s32[8]{0:T(128)S(1)}, s32[8]{0:T(128)}, u32[]{:S(2)}) copy-start(s32[8]{0:T(128)} %param.22) | copy-start | bytes 100
  30.2 11.0 %copy-start.2 = (s32[8]{0:T(128)S(1)}, s32[8]{0:T(128)}, u32[]{:S(2)}) copy-start(s32[8]{0:T(128)} %param.25) | copy-start | bytes 100
  39.3 180.2 %reduce-scatter.2.cloned.1.call-start = ((), (), s32[]{:S(2)}) async-start(), calls=%async_computation.2 | async-start | bytes 3932160 | tf_op jit(solution)/shard_map/reduce_scatter | solution.py:89
  172.2 8.0 %copy-start.6 = (bf16[1,1536,512]{1,2,0:T(8,128)(2,1)S(1)}, bf16[1,1536,512]{1,2,0:T(8,128)(2,1)}, u32[]{:S(2)}) copy-start(bf16[1,1536,512]{1,2,0:T(8,128)(2,1)} %fusion) | copy-start | bytes 4718596
  182.1 61.0 %all-gather.6.cloned.1.call-start = ((), (), s32[]{:S(2)}) async-start(), calls=%async_computation.3 | async-start | bytes 1966080 | tf_op jit(solution)/shard_map/all_gather | solution.py:101
  220.8 1.1 copy-start.4
  222.8 101.5 %all-reduce.3.cloned.1.call-start = ((), (), s32[]{:S(2)}) async-start(), calls=%async_computation.5 | async-start | bytes 1572864 | tf_op jit(solution)/shard_map/psum | solution.py:109
  245.2 5.0 %copy-start.5 = (bf16[1536,128]{0,1:T(8,128)(2,1)}, bf16[1536,128]{0,1:T(8,128)(2,1)S(1)}, u32[]{:S(2)}) copy-start(bf16[1536,128]{0,1:T(8,128)(2,1)S(1)} %fusion.4) | copy-start | bytes 1179652
  250.2 96.0 %all-gather.8.cloned.1.call-start = ((), (), s32[]{:S(2)}) async-start(), calls=%async_computation.4 | async-start | bytes 1966080 | tf_op jit(solution)/shard_map/all_gather | solution.py:107
  253.4 70.9 %copy-start.10 = (f32[128,512]{1,0:T(8,128)S(1)}, f32[128,512]{1,0:T(8,128)}, u32[]{:S(2)}) copy-start(f32[128,512]{1,0:T(8,128)} %param.28) | copy-start | bytes 786436
  255.5 80.2 %copy-start.11 = (f32[128,512]{1,0:T(8,128)S(1)}, f32[128,512]{1,0:T(8,128)}, u32[]{:S(2)}) copy-start(f32[128,512]{1,0:T(8,128)} %param.29) | copy-start | bytes 786436
  325.3 23.5 %copy-start.7 = (f32[128,512]{1,0:T(8,128)}, f32[128,512]{1,0:T(8,128)S(1)}, u32[]{:S(2)}) copy-start(f32[128,512]{1,0:T(8,128)S(1)} %sub.18) | copy-start | bytes 786436
  326.7 24.1 %copy-start.8 = (bf16[128,512]{1,0:T(8,128)(2,1)}, bf16[128,512]{1,0:T(8,128)(2,1)S(1)}, u32[]{:S(2)}) copy-start(bf16[128,512]{1,0:T(8,128)(2,1)S(1)} %fusion.6) | copy-start | bytes 393220
Sparse Core Ops, SparseCore 0:
  39.4 104.4 all-gather.3
  182.2 37.2 reduce-scatter.1
  222.9 20.1 all-gather.5
  250.3 73.9 all-reduce.2
  325.7 20.4 all-gather.7
where the time goes:
time: 360 us; the launch traced here: 359 us
  waiting for transfers between devices  235 us (65%)
  local copies, waits for them, and re-layouts  37.7 us (10%)
  matrix products  27.1 us (8%)
  other arithmetic  26.2 us (7%)
  between operations  14.4 us (4%)
  starting transfers between devices  9.34 us (3%)
  blocking collectives  8.96 us (2%)
    all_gather x1, waiting for transfers between devices, on_device(): held = lax.all_gather(mine, 'row', axis=2, tiled=True)  98.8 us
    psum x1, waiting for transfers between devices, on_device(): lax.psum((contract_rows(by_slot(col_a, own_a, live_a), factor_a), contrac...  67.4 us
    reduce_scatter x1, waiting for transfers between devices, on_device(): lax.psum_scatter(part, 'col', scatter_dimension=2, tiled=True)  35.3 us
    dot_general x2, matrix products, partial_product(): jnp.dot(trailing, spread, preferred_element_type=jnp.float32)  17 us
    all_gather x1, waiting for transfers between devices, on_device(): whole_a = lax.all_gather(col_a, 'col', axis=1, tiled=True)  13.7 us
    ppermute x7, waiting for transfers between devices, on_device(): piece = lax.ppermute(piece, ('row', 'col'), pairs)  10.8 us
    all_gather x1, blocking collectives, on_device(): top_whole = lax.all_gather(top_b, 'col', axis=0, tiled=True)  8.96 us
    ppermute x7, starting transfers between devices, on_device(): piece = lax.ppermute(piece, ('row', 'col'), pairs)  8.95 us
  transfers between devices with their start and end apart: 12, of which 7 were waited for; matrix products, arithmetic and copies ran while one was open for 9% of the time, Pallas kernels for 0%

commit v1 on v0

v1 whole, which is shorter than its diff:
```python
import functools

import jax
import jax.numpy as jnp
from jax import lax
from jax.experimental import pallas as pl
from jax.experimental.pallas import tpu as pltpu
from jax.sharding import PartitionSpec as P

MESH = pl.DeviceIdType.MESH
LANES = 128
CORES = 2
SKEW = 1
F32 = jnp.float32
BF16 = jnp.bfloat16


def contract_rows(former, latter):
    return lax.dot_general(
        former, latter, (((0,), (0,)), ((), ())), preferred_element_type=F32
    )


def times_exact(left, right):
    total = None
    for _ in range(3):
        term = left.astype(BF16)
        left = left - term.astype(F32)
        product = jnp.dot(term, right, preferred_element_type=F32)
        total = product if total is None else total + product
    return total


def kept(value, position, count):
    counts = jnp.full((1, value.shape[-1]), count, jnp.int32)
    return value * jnp.where(counts > position, 1.0, 0.0).astype(value.dtype)


class Sizes:
    def __init__(self, rows, cols, trailing, table, factor):
        self.R, self.C = rows, cols
        self.fanout = rows // cols
        self.slots = table[1]
        self.N, self.width = factor
        self.block = self.N // self.slots
        self.mrows, self.mcols = trailing
        self.row_blocks = self.mrows // self.block
        self.X = cols // CORES
        self.Y = self.X
        while rows % self.Y or self.slots % self.Y:
            self.Y -= 1
        self.Z = rows // self.Y
        self.sl = self.slots // self.Y
        self.cw = CORES * LANES
        self.W = self.width // self.cw
        self.chunks = 2 * self.W
        self.T = self.chunks * self.sl
        self.D = SKEW * (self.Z - 1) + 1
        self.pw = self.width // cols
        self.rp = self.pw // rows
        self.tile = self.mrows
        while self.tile > 512:
            self.tile //= 2
        self.G = self.width // LANES


def kernel(n, *refs):
    (
        m_hbm, rows_a, counts_a, fa_hbm, rows_b, counts_b, fb_hbm, ft_hbm, ba_hbm, bb_hbm,
        col_a_out, diag_a_out, col_b_out, top_out, diag_b_out,
        m, fa, fb, ft, ba, bb, held, rhs, acc, own, s1, r1, x2, whole_a, whole_b, fin,
        slot_a, slot_b, part_c, stage, ssend, srecv, agbuf, bsend, brecv, bag,
        diag_a, top, tsend, trecv, tt, diag_b,
        in_sem, m_sem, src_sem, lane_sem, cross_sem, up_sem, down_sem, y_sem, s1_sem,
        core_s, core_r, xs_sem, xr_sem, ws_sem, wr_sem,
        rs_s, rs_r, ag_s, ag_r, t_s, t_r, out_sem,
    ) = refs
    B = n.block
    r, c = lax.axis_index("row"), lax.axis_index("col")
    z, y = r // n.Y, r % n.Y
    x, k = c // CORES, c % CORES
    owners = [c + n.C * i for i in range(n.fanout)]
    z0 = [o // n.Y for o in owners]
    y0 = [o % n.Y for o in owners]
    src = [r == o for o in owners]
    hop = [jnp.abs(z - q) for q in z0]

    def copy_in(a, b, sem):
        cp = pltpu.make_async_copy(a, b, sem)
        cp.start()
        return cp

    def remote(a, b, s, d, dev):
        return pltpu.make_async_remote_copy(
            src_ref=a, dst_ref=b, send_sem=s, recv_sem=d, device_id=dev, device_id_type=MESH
        )

    def wait_recv(ref, sem):
        pltpu.make_async_copy(ref, ref, sem).wait()

    def source_copies(i):
        for w in range(n.chunks):
            whole = (fa_hbm, fb_hbm)[w // n.W]
            yield pltpu.make_async_copy(
                whole.at[:, pl.ds((w % n.W) * n.cw, n.cw)], held.at[w, i], src_sem.at[w]
            )

    for i in range(n.fanout):

        @pl.when(src[i])
        def _():
            for cp in source_copies(i):
                cp.start()

    load_m = [
        copy_in(m_hbm.at[:, j * B : (j + 1) * B], m.at[j], m_sem.at[j])
        for j in range(n.mcols // B)
    ]
    loads = [
        copy_in(a, b, in_sem.at[1 + j])
        for j, (a, b) in enumerate(
            ((fa_hbm, fa), (fb_hbm, fb), (ft_hbm, ft), (ba_hbm, ba), (bb_hbm, bb))
        )
    ]

    def forward(i, t):
        u = t - SKEW * hop[i]

        @pl.when(jnp.logical_and(u >= 0, u < n.T))
        def _():
            w, s = u // n.sl, u % n.sl
            piece = held.at[w, i, pl.ds(pl.multiple_of((y * n.sl + s) * B, B), B)]

            @pl.when(jnp.logical_and(src[i], s == 0))
            def _():
                pltpu.make_async_copy(
                    fa_hbm.at[:, pl.ds(0, n.cw)], held.at[w, i], src_sem.at[w]
                ).wait()

            @pl.when(jnp.logical_not(src[i]))
            def _():
                wait_recv(piece, lane_sem.at[i, u])

            @pl.when(jnp.logical_and(z >= z0[i], z < n.Z - 1))
            def _():
                remote(piece, piece, up_sem.at[i], lane_sem.at[i, u], (r + n.Y, c)).start()

            @pl.when(jnp.logical_and(z <= z0[i], z > 0))
            def _():
                remote(piece, piece, down_sem.at[i], lane_sem.at[i, u], (r - n.Y, c)).start()

            for dy in range(1, n.Y):
                to = lax.rem(y + dy, n.Y)
                dev = (z * n.Y + to, c)

                @pl.when(jnp.logical_not(jnp.logical_and(z == z0[i], to == y0[i])))
                def _():
                    remote(
                        piece, piece, y_sem.at[dy - 1, i], cross_sem.at[n.Y - dy - 1, i, u], dev
                    ).start()

                @pl.when(src[i])
                def _():
                    other = held.at[w, i, pl.ds(pl.multiple_of((to * n.sl + s) * B, B), B)]
                    remote(other, other, s1_sem.at[dy - 1, i], lane_sem.at[i, u], dev).start()

    def product(v):
        w, s = v // n.sl, v % n.sl
        first = w < n.W
        cols = []
        for i in range(n.fanout):
            for dy in range(1, n.Y):

                @pl.when(jnp.logical_not(src[i]))
                def _():
                    lane = lax.rem(y + dy, n.Y)
                    piece = held.at[w, i, pl.ds(pl.multiple_of((lane * n.sl + s) * B, B), B)]
                    wait_recv(piece, cross_sem.at[dy - 1, i, v])

        for i in range(n.fanout):
            count = jnp.where(first, counts_a[owners[i]], counts_b[owners[i]])
            for j in range(n.Y):
                q = j * n.sl + s
                row = jnp.where(first, rows_a[owners[i], q], rows_b[owners[i], q])
                block = held[w, i, pl.ds(pl.multiple_of(q * B, B), B), :]
                rhs[len(cols) * B : (len(cols) + 1) * B, :] = kept(block, q, count)
                cols.append(row * n.fanout + i)

        @pl.loop(0, n.mrows // n.tile)
        def _(step):
            at = pl.ds(pl.multiple_of(step * n.tile, n.tile), n.tile)
            left = jnp.concatenate([m[col, at, :] for col in cols], axis=1)
            part = jnp.dot(left, rhs[...], preferred_element_type=F32)

            @pl.when(s == 0)
            def _():
                acc[at, :] = part

            @pl.when(s != 0)
            def _():
                acc[at, :] += part

    def segment(start, stop):
        def body(t, carry):
            for i in range(n.fanout):
                forward(i, t)
            v = t - n.D

            @pl.when(jnp.logical_and(v >= 0, v < n.T))
            def _():
                product(v)

            return carry

        lax.fori_loop(start, stop, body, 0)

    partner = (r, c + 1 - 2 * k)
    tiles = n.mrows // n.tile

    def row_tiles(f):
        @pl.loop(0, tiles)
        def _(step):
            f(pl.ds(pl.multiple_of(step * n.tile, n.tile), n.tile))

    def core_copy(w):
        return remote(s1.at[w], r1.at[w], core_s.at[w], core_r.at[w], partner)

    def x_copy(w, dx):
        to = lax.rem(x + dx, n.X)
        return remote(
            x2.at[w, x], x2.at[w, x], xs_sem.at[w, dx - 1], xr_sem.at[w, x], (r, to * CORES + k)
        )

    def whole_copy(w):
        whole = (whole_a, whole_b)[w // n.W]
        g = (w % n.W) * CORES + k
        return remote(whole.at[g], whole.at[g], ws_sem.at[w], wr_sem.at[w], partner)

    def reduce_core(w):
        def f(at):
            s1[w, at, :] = acc[at, pl.ds(pl.multiple_of((1 - k) * LANES, LANES), LANES)].astype(BF16)
            own[at, :] = acc[at, pl.ds(pl.multiple_of(k * LANES, LANES), LANES)]

        row_tiles(f)
        core_copy(w).start()

    def reduce_x(w):
        wait_recv(r1.at[w], core_r.at[w])

        def f(at):
            x2[w, x, at, :] = (own[at, :] + r1[w, at, :].astype(F32)).astype(BF16)

        row_tiles(f)
        for dx in range(1, n.X):
            x_copy(w, dx).start()

    def finish(w):
        node = w // n.W
        whole = (whole_a, whole_b)[node]
        for dx in range(1, n.X):
            frm = lax.rem(x + dx, n.X)
            wait_recv(x2.at[w, frm], xr_sem.at[w, frm])
        g = (w % n.W) * CORES + k

        def f(at, some):
            total = x2[w, 0, at, :].astype(F32)
            for j in range(1, n.X):
                total = total + x2[w, j, at, :].astype(F32)
            if node:
                right = ft[:, pl.ds(pl.multiple_of(g * LANES, LANES), LANES)]
                left = jnp.concatenate(
                    [whole_a[j, some].reshape(n.tile, LANES) for j in range(n.G)], axis=1
                )
                total = total + jnp.dot(left, right, preferred_element_type=F32)
            value = (-total).astype(BF16).reshape(n.tile // B, B, LANES)
            whole[g, some] = value
            if node:
                @pl.when(((c * n.pw) // LANES) == g)
                def _():
                    fin[some] = value

        @pl.loop(0, tiles)
        def _(step):
            f(
                pl.ds(pl.multiple_of(step * n.tile, n.tile), n.tile),
                pl.ds(step * (n.tile // B), n.tile // B),
            )

        whole_copy(w).start()

    def gathered(w):
        whole = (whole_a, whole_b)[w // n.W]
        wait_recv(whole.at[(w % n.W) * CORES + 1 - k], wr_sem.at[w])

    def by_slot(dst, whole, rows, counts):
        for q in range(n.slots):
            for g in range(n.G):
                dst[q * B : (q + 1) * B, g * LANES : (g + 1) * LANES] = kept(
                    whole[g, rows[r, q]], q, counts[r]
                )

    group = (c * n.pw) // LANES
    inside = pl.multiple_of(lax.rem(c * n.pw, LANES), n.pw)
    group_at = pl.ds(pl.multiple_of(group * LANES, LANES), LANES)

    def share(send, sem_s, sem_r, recv):
        recv[r] = send[r]
        for dr in range(1, n.R):
            to = lax.rem(r + dr, n.R)
            remote(send.at[to], recv.at[r], sem_s.at[dr - 1], sem_r.at[r], (to, c)).start()

    def add_up(recv, sem_s, sem_r, gather_s, gather_r, bag_ref):
        for dr in range(1, n.R):
            frm = lax.rem(r + dr, n.R)
            wait_recv(recv.at[frm], sem_r.at[frm])
        total = recv[0].astype(F32)
        for j in range(1, n.R):
            total = total + recv[j].astype(F32)
        bag_ref[r] = total.astype(BF16)
        for dr in range(1, n.R):
            to = lax.rem(r + dr, n.R)
            remote(bag_ref.at[r], bag_ref.at[r], gather_s.at[dr - 1], gather_r.at[r], (to, c)).start()

    def gather_sums(bag_ref, gather_r):
        for dr in range(1, n.R):
            frm = lax.rem(r + dr, n.R)
            wait_recv(bag_ref.at[frm], gather_r.at[frm])

    def end_sends(ref_send, sem_s, bag_ref, gather_s):
        for dr in range(1, n.R):
            wait_recv(ref_send.at[0], sem_s.at[dr - 1])
            wait_recv(bag_ref.at[0], gather_s.at[dr - 1])

    def sums_a():
        for cp in loads[:3]:
            cp.wait()
        by_slot(slot_a, whole_a, rows_a, counts_a)
        for q in range(n.slots):
            part_c[q * B : (q + 1) * B, :] = kept(
                whole_a[group, rows_b[r, q]], q, counts_b[r]
            )
        copy_in(slot_a, col_a_out, out_sem.at[0])
        for j, (left, right) in enumerate(((slot_a[:, group_at], fa), (part_c[...], fb))):
            stage[...] = contract_rows(left, right[...])
            mine = stage[pl.ds(inside, n.pw), :]
            for i in range(n.R):
                ssend[i, j] = mine[i * n.rp : (i + 1) * n.rp].astype(BF16)
        share(ssend, rs_s.at[0], rs_r.at[0], srecv)

    def sums_a_add():
        add_up(srecv, rs_s.at[0], rs_r.at[0], ag_s.at[0], ag_r.at[0], agbuf)

    def tops():
        gather_sums(agbuf, ag_r.at[0])
        loads[3].wait()
        sum_a = jnp.concatenate([agbuf[i, 0] for i in range(n.R)], axis=0).astype(F32)
        sum_c = jnp.concatenate([agbuf[i, 1] for i in range(n.R)], axis=0).astype(F32)
        diag_a[...] = ba[...] - sum_a
        top[...] = (-(sum_c + times_exact(diag_a[...], ft[...]))).astype(BF16)
        copy_in(diag_a, diag_a_out, out_sem.at[1])
        copy_in(top, top_out, out_sem.at[2])
        for g in range(n.G):
            tsend[g] = top[:, g * LANES : (g + 1) * LANES]
        trecv[c] = tsend[group]
        for dc in range(1, n.C):
            to = lax.rem(c + dc, n.C)
            remote(
                tsend.at[(to * n.pw) // LANES], trecv.at[c], t_s.at[dc - 1], t_r.at[c], (r, to)
            ).start()

    def tops_in():
        for dc in range(1, n.C):
            frm = lax.rem(c + dc, n.C)
            wait_recv(trecv.at[frm], t_r.at[frm])
        columns = jnp.concatenate([trecv[i] for i in range(n.C)], axis=0)
        tt[...] = contract_rows(columns, ft[...])

    events = {}

    def after(t, f, *args):
        events.setdefault(t, []).append(functools.partial(f, *args))

    end = n.T + n.D
    for w in range(n.chunks):
        done = (w + 1) * n.sl + n.D
        after(done, reduce_core, w)
        if w < n.chunks - 1:
            after(min(done + 1, end), reduce_x, w)
            after(min(done + 5, end), finish, w)
            after(min(done + 6, end), gathered, w)
    ready = n.W * n.sl + n.D + 6
    after(min(ready, end), sums_a)
    after(min(ready + 2, end), sums_a_add)
    after(min(ready + 4, end), tops)
    after(min(ready + 6, end), tops_in)
    at = 0
    for t in sorted(set(events) | {n.D, end}):
        if t > at:
            segment(at, t)
            at = t
        if t == n.D:
            for cp in load_m:
                cp.wait()
        for f in events.get(t, ()):
            f()
    last = n.chunks - 1
    reduce_x(last)
    finish(last)
    if n.pw != LANES:
        gathered(last)
    for q in range(n.slots):
        row = rows_b[r, q]
        value = fin[row] if n.pw == LANES else whole_b[group, row]
        part_c[q * B : (q + 1) * B, :] = kept(value, q, counts_b[r])
    stage[...] = contract_rows(part_c[...], fb[...])
    mine = stage[pl.ds(inside, n.pw), :]
    for i in range(n.R):
        bsend[i] = mine[i * n.rp : (i + 1) * n.rp].astype(BF16)
    share(bsend, rs_s.at[1], rs_r.at[1], brecv)
    if n.pw == LANES:
        gathered(last)
    by_slot(slot_b, whole_b, rows_b, counts_b)
    copy_in(slot_b, col_b_out, out_sem.at[3])
    add_up(brecv, rs_s.at[1], rs_r.at[1], ag_s.at[1], ag_r.at[1], bag)
    for i in range(n.fanout):
        share_of = held.at[:, i, pl.ds(0, n.sl * B)]

        @pl.when(jnp.logical_and(z >= z0[i], z < n.Z - 1))
        def _():
            wait_recv(share_of, up_sem.at[i])

        @pl.when(jnp.logical_and(z <= z0[i], z > 0))
        def _():
            wait_recv(share_of, down_sem.at[i])

        for dy in range(1, n.Y):
            to = lax.rem(y + dy, n.Y)

            @pl.when(jnp.logical_not(jnp.logical_and(z == z0[i], to == y0[i])))
            def _():
                wait_recv(share_of, y_sem.at[dy - 1, i])

            @pl.when(src[i])
            def _():
                wait_recv(share_of, s1_sem.at[dy - 1, i])

    for w in range(n.chunks):
        wait_recv(s1.at[w], core_s.at[w])
        wait_recv(s1.at[w], ws_sem.at[w])
        for dx in range(1, n.X):
            wait_recv(s1.at[w], xs_sem.at[w, dx - 1])
    for dc in range(1, n.C):
        wait_recv(tsend.at[0], t_s.at[dc - 1])
    loads[4].wait()
    gather_sums(bag, ag_r.at[1])
    sum_b = jnp.concatenate([bag[i] for i in range(n.R)], axis=0).astype(F32)
    diag_b[...] = bb[...] - sum_b - tt[pl.ds(inside, n.pw), :]
    copy_in(diag_b, diag_b_out, out_sem.at[4])
    end_sends(ssend, rs_s.at[0], agbuf, ag_s.at[0])
    end_sends(bsend, rs_s.at[1], bag, ag_s.at[1])
    for j, (a, b) in enumerate(
        (
            (slot_a, col_a_out),
            (diag_a, diag_a_out),
            (top, top_out),
            (slot_b, col_b_out),
            (diag_b, diag_b_out),
        )
    ):
        pltpu.make_async_copy(a, b, out_sem.at[j]).wait()


def solution(mesh):
    R, C = mesh.shape["row"], mesh.shape["col"]

    def on_device(trailing, rows_a, counts_a, factor_a, rows_b, counts_b, factor_b, factor_top, base_a, base_b):
        n = Sizes(R, C, trailing.shape, rows_a.shape, factor_a.shape)
        any_ = pl.BlockSpec(memory_space=pl.ANY)
        smem = pl.BlockSpec(memory_space=pltpu.SMEM)
        vm = pltpu.VMEM
        half = (n.mrows, LANES)
        blocks = (n.row_blocks, n.block, LANES)
        dma = pltpu.SemaphoreType.DMA
        shape = jax.ShapeDtypeStruct
        scratch = [
            vm((n.mcols // n.block, n.mrows, n.block), BF16),
            vm(factor_a.shape, BF16),
            vm(factor_b.shape, BF16),
            vm(factor_top.shape, BF16),
            vm(base_a.shape, F32),
            vm(base_b.shape, F32),
            vm((n.chunks, n.fanout, n.N, n.cw), BF16),
            vm((n.fanout * n.Y * n.block, n.cw), BF16),
            vm((n.mrows, n.cw), F32),
            vm(half, F32),
            vm((n.chunks,) + half, BF16),
            vm((n.chunks,) + half, BF16),
            vm((n.chunks, n.X) + half, BF16),
            vm((n.G,) + blocks, BF16),
            vm((n.G,) + blocks, BF16),
            vm(blocks, BF16),
            vm(factor_a.shape, BF16),
            vm(factor_b.shape, BF16),
            vm((n.N, LANES), BF16),
            vm((LANES, n.width), F32),
            vm((n.R, 2, n.rp, n.width), BF16),
            vm((n.R, 2, n.rp, n.width), BF16),
            vm((n.R, 2, n.rp, n.width), BF16),
            vm((n.R, n.rp, n.width), BF16),
            vm((n.R, n.rp, n.width), BF16),
            vm((n.R, n.rp, n.width), BF16),
            vm((n.pw, n.width), F32),
            vm((n.pw, n.width), BF16),
            vm((n.G, n.pw, LANES), BF16),
            vm((n.C, n.pw, LANES), BF16),
            vm((LANES, n.width), F32),
            vm((n.pw, n.width), F32),
            dma((6,)),
            dma((n.mcols // n.block,)),
            dma((n.chunks,)),
            dma((n.fanout, n.T)),
            dma((n.Y - 1, n.fanout, n.T)),
            dma((n.fanout,)),
            dma((n.fanout,)),
            dma((n.Y - 1, n.fanout)),
            dma((n.Y - 1, n.fanout)),
            dma((n.chunks,)),
            dma((n.chunks,)),
            dma((n.chunks, n.X - 1)),
            dma((n.chunks, n.X)),
            dma((n.chunks,)),
            dma((n.chunks,)),
            dma((2, n.R - 1)),
            dma((2, n.R)),
            dma((2, n.R - 1)),
            dma((2, n.R)),
            dma((n.C - 1,)),
            dma((n.C,)),
            dma((5,)),
        ]
        return pl.pallas_call(
            functools.partial(kernel, n),
            out_shape=(
                shape(factor_a.shape, BF16),
                shape((n.pw, n.width), F32),
                shape(factor_b.shape, BF16),
                shape((n.pw, n.width), BF16),
                shape((n.pw, n.width), F32),
            ),
            in_specs=[any_, smem, smem, any_, smem, smem, any_, any_, any_, any_],
            out_specs=(any_,) * 5,
            scratch_shapes=scratch,
            compiler_params=pltpu.CompilerParams(
                has_side_effects=True, vmem_limit_bytes=60 << 20
            ),
        )(trailing, rows_a, counts_a, factor_a, rows_b, counts_b, factor_b, factor_top, base_a, base_b)

    in_specs = (
        P("row", "col"),
        P(),
        P(),
        P("row", None),
        P(),
        P(),
        P("row", None),
        P(),
        P("col", None),
        P("col", None),
    )
    out_specs = (P("row", None), P("col", None), P("row", None), P("col", None), P("col", None))
    return jax.shard_map(
        on_device, mesh=mesh, in_specs=in_specs, out_specs=out_specs, check_vma=False
    )
```

time: 360 us -> 148 us (0.41)
  waiting for transfers between devices: 235 us -> 0 us
  Pallas kernels: 0 us -> 139 us
  local copies, waits for them, and re-layouts: 37.7 us -> 6 us
  matrix products: 27.1 us -> 0 us
  other arithmetic: 26.2 us -> 0 us
  between operations: 14.4 us -> 0.66 us
  starting transfers between devices: 9.34 us -> 0 us
  blocking collectives: 8.96 us -> 0 us
    pallas_call x0 -> x1, Pallas kernels: none -> 139 us  [on_device(): pl.pallas_call(functools.partial(kernel, n), out_shape=(shape(factor_a.sh...]
    all_gather x3 -> x0, waiting for transfers between devices: 121 us -> none  [the longest x1 98.8 us: on_device(): held = lax.all_gather(mine, 'row', axis=2, tiled=True)]
    psum x1 -> x0, waiting for transfers between devices: 67.4 us -> none  [on_device(): lax.psum((contract_rows(by_slot(col_a, own_a, live_a), factor_a), contrac...]
    reduce_scatter x1 -> x0, waiting for transfers between devices: 35.3 us -> none  [on_device(): lax.psum_scatter(part, 'col', scatter_dimension=2, tiled=True)]
    dot_general x8 -> x0, matrix products: 27.1 us -> none  [the longest x2 17 us: partial_product(): jnp.dot(trailing, spread, preferred_element_type=jnp.float32)]
    gather x11 -> x0, local copies, waits for them, and re-layouts: 17.9 us -> none  [the longest x2 8.76 us: partial_product(): jnp.take(held[node].reshape(fanout * slots, block, width), source, axis=0)]
    ppermute x7 -> x0, waiting for transfers between devices: 10.8 us -> none  [on_device(): piece = lax.ppermute(piece, ('row', 'col'), pairs)]
    all_gather x1 -> x0, blocking collectives: 8.96 us -> none  [on_device(): top_whole = lax.all_gather(top_b, 'col', axis=0, tiled=True)]
  transfers between devices with their start and end apart: 12 -> 0, of which waited for: 7 -> 0; matrix products, arithmetic and copies ran while one was open for 9% -> 0% of each run, Pallas kernels for 0% -> 0%
where the time goes in v1:
time: 148 us; the launch traced here: 146 us
  Pallas kernels  139 us (94%)
  local copies, waits for them, and re-layouts  6 us (4%)
    pallas_call x1, Pallas kernels, on_device(): pl.pallas_call(functools.partial(kernel, n), out_shape=(shape(factor_a.sh...  139 us
    unnamed x13, local copies, waits for them, and re-layouts  6 us

profile of v1, /device:TPU:1, one launch (start us, length us, event | category | flops | bytes accessed | tf_op | source)
XLA Modules:
  0.0 146.0 jit_solution(16678693847544830002)
XLA Ops:
  0.6 139.4 %shard_map.137 = (bf16[1536,512]{1,0:T(8,128)(2,1)}, f32[128,512]{1,0:T(8,128)}, bf16[1536,512]{1,0:T(8,128)(2,1)}, bf16[128,512]{1,0:T(8,128)(2,1)}, f32[128,512]{1,0:T(8,128)}) custom-call(bf16[1536,3072]{1,0:T(8,128)(2,1)} %refs_0_.1, s32[8,12]{1,0:T(8,128)} %refs_1_.1, s32[8]{0:T(128)} %refs_2_.1, bf16[1536,512]{1,0:T(8,128)(2,1)} %refs_3_.1, ...), custom_call_target="tpu_custom_call" | custom-call | tf_op jit(solution)/shard_map/pallas_call | solution.py:541
  140.0 0.0 copy-start.2
  140.0 0.0 copy-start
  140.0 2.8 %copy.20 = bf16[1536,512]{1,0:T(8,128)(2,1)} copy(bf16[1536,512]{1,0:T(8,128)(2,1)} %get-tuple-element.10) | data formatting | bytes 3145728
  142.8 0.0 copy-done.2
  142.8 0.7 copy.21
  143.5 0.0 copy-done
  143.5 0.0 copy-start.3
  143.5 0.0 copy-start.1
  143.5 1.1 copy.22
  144.7 0.0 copy-done.3
  144.7 0.7 copy.23
  145.3 0.0 copy-done.1
  145.3 0.7 copy.24
Async XLA Ops:
  140.0 2.8 %copy-start.2 = (f32[128,512]{1,0:T(8,128)S(1)}, f32[128,512]{1,0:T(8,128)}, u32[]{:S(2)}) copy-start(f32[128,512]{1,0:T(8,128)} %get-tuple-element.11) | copy-start | bytes 786436
  140.0 3.5 %copy-start = (bf16[1536,512]{1,0:T(8,128)(2,1)S(1)}, bf16[1536,512]{1,0:T(8,128)(2,1)}, u32[]{:S(2)}) copy-start(bf16[1536,512]{1,0:T(8,128)(2,1)} %get-tuple-element.12) | copy-start | bytes 4718596
  143.5 1.1 copy-start.3
  143.5 1.8 %copy-start.1 = (f32[128,512]{1,0:T(8,128)S(1)}, f32[128,512]{1,0:T(8,128)}, u32[]{:S(2)}) copy-start(f32[128,512]{1,0:T(8,128)} %get-tuple-element.14) | copy-start | bytes 786436

commit v2 on v1

--- a/solution.py
+++ b/solution.py
@@ -10,7 +10,10 @@
 MESH = pl.DeviceIdType.MESH
 LANES = 128
 CORES = 2
-SKEW = 1
+PARTS = 2
+SKEW = 3
+CROSS = 4
+AHEAD = 4
 F32 = jnp.float32
 BF16 = jnp.bfloat16
 
@@ -54,25 +57,35 @@
         self.cw = CORES * LANES
         self.W = self.width // self.cw
         self.chunks = 2 * self.W
-        self.T = self.chunks * self.sl
-        self.D = SKEW * (self.Z - 1) + 1
+        self.per = self.sl * PARTS
+        self.T = self.chunks * self.per
+        self.piece = self.block // PARTS
+        self.D = SKEW * (self.Z - 1) + CROSS
         self.pw = self.width // cols
         self.rp = self.pw // rows
         self.tile = self.mrows
         while self.tile > 512:
             self.tile //= 2
         self.G = self.width // LANES
+        self.H = self.cw // LANES
+        self.half = self.mrows // CORES
+        self.half_blocks = self.row_blocks // CORES
+        self.htile = self.half // 2
+
+    def group(self, w, h):
+        g = w % self.W + self.W * h
+        return g, g * LANES // (self.pw * CORES)
 
 
 def kernel(n, *refs):
     (
         m_hbm, rows_a, counts_a, fa_hbm, rows_b, counts_b, fb_hbm, ft_hbm, ba_hbm, bb_hbm,
         col_a_out, diag_a_out, col_b_out, top_out, diag_b_out,
-        m, fa, fb, ft, ba, bb, held, rhs, acc, own, s1, r1, x2, whole_a, whole_b, fin,
-        slot_a, slot_b, part_c, stage, ssend, srecv, agbuf, bsend, brecv, bag,
+        m, fa, fb, ft, ba, bb, held, rhs, acc, own, s1, r1, x2s, x2r, whole_a, whole_b, fin,
+        slot_a, slot_b, part_a, part_c, stage, ssend, srecv, agbuf, bsend, brecv, bag,
         diag_a, top, tsend, trecv, tt, diag_b,
         in_sem, m_sem, src_sem, lane_sem, cross_sem, up_sem, down_sem, y_sem, s1_sem,
-        core_s, core_r, xs_sem, xr_sem, ws_sem, wr_sem,
+        core_s, core_r, xs_sem, xr_sem, xo_s, xo_r, ws_sem, wr_sem, fin_s, fin_r,
         rs_s, rs_r, ag_s, ag_r, t_s, t_r, out_sem,
     ) = refs
     B = n.block
@@ -101,9 +114,13 @@
     def source_copies(i):
         for w in range(n.chunks):
             whole = (fa_hbm, fb_hbm)[w // n.W]
-            yield pltpu.make_async_copy(
-                whole.at[:, pl.ds((w % n.W) * n.cw, n.cw)], held.at[w, i], src_sem.at[w]
-            )
+            for j in range(n.Y):
+                for h in range(n.H):
+                    yield pltpu.make_async_copy(
+                        whole.at[pl.ds(j * n.per, n.per), :, pl.ds(n.group(w, h)[0] * LANES, LANES)],
+                        held.at[i, j, pl.ds(w * n.per, n.per), :, pl.ds(h * LANES, LANES)],
+                        src_sem.at[w, j, h],
+                    )
 
     for i in range(n.fanout):
 
@@ -123,19 +140,42 @@
         )
     ]
 
+    def to_lane(i, u):
+        for dy in range(1, n.Y):
+            to = lax.rem(y + dy, n.Y)
+            other = held.at[i, to, u]
+            dev = (z * n.Y + to, c)
+            remote(other, other, s1_sem.at[dy - 1, i], lane_sem.at[i, u], dev).start()
+
+    barrier = pltpu.get_barrier_semaphore()
+    peers = [(lax.rem(r + dr, n.R), c) for dr in range(1, n.R)]
+    peers += [(r, lax.rem(c + dc, n.C)) for dc in range(1, n.C)]
+    for dev in peers:
+        pl.semaphore_signal(barrier, inc=1, device_id=dev, device_id_type=MESH)
+    pl.semaphore_wait(barrier, len(peers))
+    for i in range(n.fanout):
+
+        @pl.when(src[i])
+        def _():
+            for cp in source_copies(i):
+                cp.wait()
+            for u in range(AHEAD):
+                to_lane(i, u)
+
     def forward(i, t):
         u = t - SKEW * hop[i]
 
         @pl.when(jnp.logical_and(u >= 0, u < n.T))
         def _():
-            w, s = u // n.sl, u % n.sl
-            piece = held.at[w, i, pl.ds(pl.multiple_of((y * n.sl + s) * B, B), B)]
-
-            @pl.when(jnp.logical_and(src[i], s == 0))
-            def _():
-                pltpu.make_async_copy(
-                    fa_hbm.at[:, pl.ds(0, n.cw)], held.at[w, i], src_sem.at[w]
-                ).wait()
+            piece = held.at[i, y, u]
+
+            @pl.when(src[i])
+            def _():
+                later = u + AHEAD
+
+                @pl.when(later < n.T)
+                def _():
+                    to_lane(i, later)
 
             @pl.when(jnp.logical_not(src[i]))
             def _():
@@ -151,38 +191,36 @@
 
             for dy in range(1, n.Y):
                 to = lax.rem(y + dy, n.Y)
-                dev = (z * n.Y + to, c)
 
                 @pl.when(jnp.logical_not(jnp.logical_and(z == z0[i], to == y0[i])))
                 def _():
                     remote(
-                        piece, piece, y_sem.at[dy - 1, i], cross_sem.at[n.Y - dy - 1, i, u], dev
+                        piece,
+                        piece,
+                        y_sem.at[dy - 1, i],
+                        cross_sem.at[n.Y - dy - 1, i, u],
+                        (z * n.Y + to, c),
                     ).start()
 
-                @pl.when(src[i])
-                def _():
-                    other = held.at[w, i, pl.ds(pl.multiple_of((to * n.sl + s) * B, B), B)]
-                    remote(other, other, s1_sem.at[dy - 1, i], lane_sem.at[i, u], dev).start()
-
     def product(v):
-        w, s = v // n.sl, v % n.sl
-        first = w < n.W
+        s = lax.rem(v, n.sl)
+        first = v < n.W * n.sl
         cols = []
         for i in range(n.fanout):
             for dy in range(1, n.Y):
 
                 @pl.when(jnp.logical_not(src[i]))
                 def _():
-                    lane = lax.rem(y + dy, n.Y)
-                    piece = held.at[w, i, pl.ds(pl.multiple_of((lane * n.sl + s) * B, B), B)]
-                    wait_recv(piece, cross_sem.at[dy - 1, i, v])
+                    for h in range(PARTS):
+                        u = v * PARTS + h
+                        wait_recv(held.at[i, lax.rem(y + dy, n.Y), u], cross_sem.at[dy - 1, i, u])
 
         for i in range(n.fanout):
             count = jnp.where(first, counts_a[owners[i]], counts_b[owners[i]])
             for j in range(n.Y):
                 q = j * n.sl + s
                 row = jnp.where(first, rows_a[owners[i], q], rows_b[owners[i], q])
-                block = held[w, i, pl.ds(pl.multiple_of(q * B, B), B), :]
+                block = held[i, j, pl.ds(v * PARTS, PARTS)].reshape(B, n.cw)
                 rhs[len(cols) * B : (len(cols) + 1) * B, :] = kept(block, q, count)
                 cols.append(row * n.fanout + i)
 
@@ -204,93 +242,136 @@
         def body(t, carry):
             for i in range(n.fanout):
                 forward(i, t)
-            v = t - n.D
-
-            @pl.when(jnp.logical_and(v >= 0, v < n.T))
-            def _():
-                product(v)
+            late = t - n.D + 1
+
+            @pl.when(jnp.logical_and(late > 0, lax.rem(late, PARTS) == 0))
+            def _():
+                product(lax.div(late, PARTS) - 1)
 
             return carry
 
         lax.fori_loop(start, stop, body, 0)
 
     partner = (r, c + 1 - 2 * k)
-    tiles = n.mrows // n.tile
-
-    def row_tiles(f):
-        @pl.loop(0, tiles)
+
+    mine_rows = pl.ds(pl.multiple_of(k * n.half, n.half), n.half)
+    mine_blocks = pl.ds(k * n.half_blocks, n.half_blocks)
+    other_blocks = pl.ds((1 - k) * n.half_blocks, n.half_blocks)
+    wholes = (whole_a, whole_b)
+
+    def half_tiles(f):
+        @pl.loop(0, n.half // n.htile)
         def _(step):
-            f(pl.ds(pl.multiple_of(step * n.tile, n.tile), n.tile))
-
-    def core_copy(w):
-        return remote(s1.at[w], r1.at[w], core_s.at[w], core_r.at[w], partner)
-
-    def x_copy(w, dx):
-        to = lax.rem(x + dx, n.X)
-        return remote(
-            x2.at[w, x], x2.at[w, x], xs_sem.at[w, dx - 1], xr_sem.at[w, x], (r, to * CORES + k)
-        )
-
-    def whole_copy(w):
-        whole = (whole_a, whole_b)[w // n.W]
-        g = (w % n.W) * CORES + k
-        return remote(whole.at[g], whole.at[g], ws_sem.at[w], wr_sem.at[w], partner)
+            f(pl.multiple_of(step * n.htile, n.htile))
+
+    def at_owner(w, f, g=None):
+        for h in range(n.H):
+            index, chip = n.group(w, h)
+            if f is not None:
+
+                @pl.when(x == chip)
+                def _():
+                    f(h, index)
+
+            if g is not None:
+
+                @pl.when(x != chip)
+                def _():
+                    g(h, index)
 
     def reduce_core(w):
         def f(at):
-            s1[w, at, :] = acc[at, pl.ds(pl.multiple_of((1 - k) * LANES, LANES), LANES)].astype(BF16)
-            own[at, :] = acc[at, pl.ds(pl.multiple_of(k * LANES, LANES), LANES)]
-
-        row_tiles(f)
-        core_copy(w).start()
+            theirs = pl.ds(pl.multiple_of((1 - k) * n.half + at, n.htile), n.htile)
+            ours = pl.ds(pl.multiple_of(k * n.half + at, n.htile), n.htile)
+            s1[w, pl.ds(at, n.htile), :] = acc[theirs, :].astype(BF16)
+            own[pl.ds(at, n.htile), :] = acc[ours, :]
+
+        half_tiles(f)
+        remote(s1.at[w], r1.at[w], core_s.at[w], core_r.at[w], partner).start()
 
     def reduce_x(w):
         wait_recv(r1.at[w], core_r.at[w])
 
         def f(at):
-            x2[w, x, at, :] = (own[at, :] + r1[w, at, :].astype(F32)).astype(BF16)
-
-        row_tiles(f)
-        for dx in range(1, n.X):
-            x_copy(w, dx).start()
+            rows = pl.ds(at, n.htile)
+            total = own[rows, :] + r1[w, rows, :].astype(F32)
+            own[rows, :] = total
+            for h in range(n.H):
+                x2s[w, h, rows, :] = total[:, h * LANES : (h + 1) * LANES].astype(BF16)
+
+        half_tiles(f)
+
+        def send(h, g):
+            chip = n.group(w, h)[1]
+            remote(
+                x2s.at[w, h], x2r.at[w, h, x], xs_sem.at[w, h], xr_sem.at[w, h, x], (r, chip * CORES + k)
+            ).start()
+
+        at_owner(w, None, send)
+
+    def to_partner(w, h, g):
+        part = wholes[w // n.W].at[g, mine_blocks]
+        remote(part, part, ws_sem.at[w, h], wr_sem.at[w, h], partner).start()
 
     def finish(w):
         node = w // n.W
-        whole = (whole_a, whole_b)[node]
-        for dx in range(1, n.X):
-            frm = lax.rem(x + dx, n.X)
-            wait_recv(x2.at[w, frm], xr_sem.at[w, frm])
-        g = (w % n.W) * CORES + k
-
-        def f(at, some):
-            total = x2[w, 0, at, :].astype(F32)
-            for j in range(1, n.X):
-                total = total + x2[w, j, at, :].astype(F32)
+
+        def own_group(h, g):
+            for dx in range(1, n.X):
+                frm = lax.rem(x + dx, n.X)
+                wait_recv(x2r.at[w, h, frm], xr_sem.at[w, h, frm])
+
+            def f(at):
+                rows = pl.ds(at, n.htile)
+                count = n.htile // B
+                some = pl.ds(k * n.half_blocks + lax.div(at, B), count)
+                total = own[rows, h * LANES : (h + 1) * LANES]
+                for dx in range(1, n.X):
+                    total = total + x2r[w, h, lax.rem(x + dx, n.X), rows, :].astype(F32)
+                if node:
+                    left = jnp.concatenate(
+                        [whole_a[j, some].reshape(n.htile, LANES) for j in range(n.G)], axis=1
+                    )
+                    right = ft[:, g * LANES : (g + 1) * LANES]
+                    total = total + jnp.dot(left, right, preferred_element_type=F32)
+                value = (-total).astype(BF16).reshape(count, B, LANES)
+                wholes[node][g, some] = value
+                if node:
+                    fin[w % n.W, some] = value
+
+            half_tiles(f)
             if node:
-                right = ft[:, pl.ds(pl.multiple_of(g * LANES, LANES), LANES)]
-                left = jnp.concatenate(
-                    [whole_a[j, some].reshape(n.tile, LANES) for j in range(n.G)], axis=1
-                )
-                total = total + jnp.dot(left, right, preferred_element_type=F32)
-            value = (-total).astype(BF16).reshape(n.tile // B, B, LANES)
-            whole[g, some] = value
-            if node:
-                @pl.when(((c * n.pw) // LANES) == g)
-                def _():
-                    fin[some] = value
-
-        @pl.loop(0, tiles)
-        def _(step):
-            f(
-                pl.ds(pl.multiple_of(step * n.tile, n.tile), n.tile),
-                pl.ds(step * (n.tile // B), n.tile // B),
-            )
-
-        whole_copy(w).start()
+                part = fin.at[w % n.W, mine_blocks]
+                remote(part, part, fin_s.at[w % n.W], fin_r.at[w % n.W], partner).start()
+            part = wholes[node].at[g, mine_blocks]
+            for dx in range(1, n.X):
+                to = lax.rem(x + dx, n.X)
+                remote(
+                    part, part, xo_s.at[w, h, dx - 1], xo_r.at[w, h], (r, to * CORES + k)
+                ).start()
+            to_partner(w, h, g)
+
+        at_owner(w, own_group)
+
+    def relay(w):
+        def f(h, g):
+            wait_recv(wholes[w // n.W].at[g, mine_blocks], xo_r.at[w, h])
+            to_partner(w, h, g)
+
+        at_owner(w, None, f)
 
     def gathered(w):
-        whole = (whole_a, whole_b)[w // n.W]
-        wait_recv(whole.at[(w % n.W) * CORES + 1 - k], wr_sem.at[w])
+        for h in range(n.H):
+            g = n.group(w, h)[0]
+            wait_recv(wholes[w // n.W].at[g, other_blocks], wr_sem.at[w, h])
+
+    def fins():
+        for w in range(n.W):
+
+            def f(h, g):
+                wait_recv(fin.at[w, other_blocks], fin_r.at[w])
+
+            at_owner(w, f)
 
     def by_slot(dst, whole, rows, counts):
         for q in range(n.slots):
@@ -301,7 +382,6 @@
 
     group = (c * n.pw) // LANES
     inside = pl.multiple_of(lax.rem(c * n.pw, LANES), n.pw)
-    group_at = pl.ds(pl.multiple_of(group * LANES, LANES), LANES)
 
     def share(send, sem_s, sem_r, recv):
         recv[r] = send[r]
@@ -334,14 +414,12 @@
     def sums_a():
         for cp in loads[:3]:
             cp.wait()
-        by_slot(slot_a, whole_a, rows_a, counts_a)
         for q in range(n.slots):
-            part_c[q * B : (q + 1) * B, :] = kept(
-                whole_a[group, rows_b[r, q]], q, counts_b[r]
-            )
-        copy_in(slot_a, col_a_out, out_sem.at[0])
-        for j, (left, right) in enumerate(((slot_a[:, group_at], fa), (part_c[...], fb))):
-            stage[...] = contract_rows(left, right[...])
+            at = slice(q * B, (q + 1) * B)
+            part_a[at, :] = kept(whole_a[group, rows_a[r, q]], q, counts_a[r])
+            part_c[at, :] = kept(whole_a[group, rows_b[r, q]], q, counts_b[r])
+        for j, (left, right) in enumerate(((part_a[...], fa), (part_c[...], fb))):
+            stage[...] = contract_rows(left, right[...].reshape(n.N, n.width))
             mine = stage[pl.ds(inside, n.pw), :]
             for i in range(n.R):
                 ssend[i, j] = mine[i * n.rp : (i + 1) * n.rp].astype(BF16)
@@ -378,21 +456,19 @@
     events = {}
 
     def after(t, f, *args):
-        events.setdefault(t, []).append(functools.partial(f, *args))
+        events.setdefault(min(t, end), []).append(functools.partial(f, *args))
 
     end = n.T + n.D
-    for w in range(n.chunks):
-        done = (w + 1) * n.sl + n.D
+    last = n.chunks - 1
+    for w in range(last):
+        done = (w + 1) * n.per + n.D
         after(done, reduce_core, w)
-        if w < n.chunks - 1:
-            after(min(done + 1, end), reduce_x, w)
-            after(min(done + 5, end), finish, w)
-            after(min(done + 6, end), gathered, w)
-    ready = n.W * n.sl + n.D + 6
-    after(min(ready, end), sums_a)
-    after(min(ready + 2, end), sums_a_add)
-    after(min(ready + 4, end), tops)
-    after(min(ready + 6, end), tops_in)
+        after(done + 1 * PARTS, reduce_x, w)
+        after(done + 4 * PARTS, finish, w)
+        if w < last - 1:
+            after(done + 7 * PARTS, relay, w)
+            after(done + 8 * PARTS, gathered, w)
+    after(n.W * n.per + n.D + 8 * PARTS, sums_a)
     at = 0
     for t in sorted(set(events) | {n.D, end}):
         if t > at:
@@ -403,27 +479,33 @@
                 cp.wait()
         for f in events.get(t, ()):
             f()
-    last = n.chunks - 1
+    reduce_core(last)
+    relay(last - 1)
+    sums_a_add()
     reduce_x(last)
+    tops()
+    by_slot(slot_a, whole_a, rows_a, counts_a)
+    copy_in(slot_a, col_a_out, out_sem.at[0])
     finish(last)
-    if n.pw != LANES:
-        gathered(last)
+    fins()
     for q in range(n.slots):
-        row = rows_b[r, q]
-        value = fin[row] if n.pw == LANES else whole_b[group, row]
-        part_c[q * B : (q + 1) * B, :] = kept(value, q, counts_b[r])
-    stage[...] = contract_rows(part_c[...], fb[...])
+        part_c[q * B : (q + 1) * B, :] = kept(
+            fin[lax.rem(group, n.W), rows_b[r, q]], q, counts_b[r]
+        )
+    stage[...] = contract_rows(part_c[...], fb[...].reshape(n.N, n.width))
     mine = stage[pl.ds(inside, n.pw), :]
     for i in range(n.R):
         bsend[i] = mine[i * n.rp : (i + 1) * n.rp].astype(BF16)
     share(bsend, rs_s.at[1], rs_r.at[1], brecv)
-    if n.pw == LANES:
-        gathered(last)
+    tops_in()
+    gathered(last - 1)
+    relay(last)
+    add_up(brecv, rs_s.at[1], rs_r.at[1], ag_s.at[1], ag_r.at[1], bag)
+    gathered(last)
     by_slot(slot_b, whole_b, rows_b, counts_b)
     copy_in(slot_b, col_b_out, out_sem.at[3])
-    add_up(brecv, rs_s.at[1], rs_r.at[1], ag_s.at[1], ag_r.at[1], bag)
     for i in range(n.fanout):
-        share_of = held.at[:, i, pl.ds(0, n.sl * B)]
+        share_of = held.at[i, 0]
 
         @pl.when(jnp.logical_and(z >= z0[i], z < n.Z - 1))
         def _():
@@ -446,9 +528,19 @@
 
     for w in range(n.chunks):
         wait_recv(s1.at[w], core_s.at[w])
-        wait_recv(s1.at[w], ws_sem.at[w])
-        for dx in range(1, n.X):
-            wait_recv(s1.at[w], xs_sem.at[w, dx - 1])
+
+        def sent(h, g):
+            for dx in range(1, n.X):
+                wait_recv(x2s.at[w, h], xo_s.at[w, h, dx - 1])
+            if w >= n.W:
+                wait_recv(x2s.at[w, h], fin_s.at[w % n.W])
+
+        def sent_part(h, g):
+            wait_recv(x2s.at[w, h], xs_sem.at[w, h])
+
+        at_owner(w, sent, sent_part)
+        for h in range(n.H):
+            wait_recv(x2s.at[w, h], ws_sem.at[w, h])
     for dc in range(1, n.C):
         wait_recv(tsend.at[0], t_s.at[dc - 1])
     loads[4].wait()
@@ -478,29 +570,30 @@
         any_ = pl.BlockSpec(memory_space=pl.ANY)
         smem = pl.BlockSpec(memory_space=pltpu.SMEM)
         vm = pltpu.VMEM
-        half = (n.mrows, LANES)
         blocks = (n.row_blocks, n.block, LANES)
         dma = pltpu.SemaphoreType.DMA
         shape = jax.ShapeDtypeStruct
         scratch = [
             vm((n.mcols // n.block, n.mrows, n.block), BF16),
-            vm(factor_a.shape, BF16),
-            vm(factor_b.shape, BF16),
+            vm((n.slots * PARTS, n.piece, n.width), BF16),
+            vm((n.slots * PARTS, n.piece, n.width), BF16),
             vm(factor_top.shape, BF16),
             vm(base_a.shape, F32),
             vm(base_b.shape, F32),
-            vm((n.chunks, n.fanout, n.N, n.cw), BF16),
+            vm((n.fanout, n.Y, n.T, n.piece, n.cw), BF16),
             vm((n.fanout * n.Y * n.block, n.cw), BF16),
             vm((n.mrows, n.cw), F32),
-            vm(half, F32),
-            vm((n.chunks,) + half, BF16),
-            vm((n.chunks,) + half, BF16),
-            vm((n.chunks, n.X) + half, BF16),
+            vm((n.half, n.cw), F32),
+            vm((n.chunks, n.half, n.cw), BF16),
+            vm((n.chunks, n.half, n.cw), BF16),
+            vm((n.chunks, n.H, n.half, LANES), BF16),
+            vm((n.chunks, n.H, n.X, n.half, LANES), BF16),
             vm((n.G,) + blocks, BF16),
             vm((n.G,) + blocks, BF16),
-            vm(blocks, BF16),
+            vm((n.W,) + blocks, BF16),
             vm(factor_a.shape, BF16),
             vm(factor_b.shape, BF16),
+            vm((n.N, LANES), BF16),
             vm((n.N, LANES), BF16),
             vm((LANES, n.width), F32),
             vm((n.R, 2, n.rp, n.width), BF16),
@@ -517,7 +610,7 @@
             vm((n.pw, n.width), F32),
             dma((6,)),
             dma((n.mcols // n.block,)),
-            dma((n.chunks,)),
+            dma((n.chunks, n.Y, n.H)),
             dma((n.fanout, n.T)),
             dma((n.Y - 1, n.fanout, n.T)),
             dma((n.fanout,)),
@@ -526,10 +619,14 @@
             dma((n.Y - 1, n.fanout)),
             dma((n.chunks,)),
             dma((n.chunks,)),
-            dma((n.chunks, n.X - 1)),
-            dma((n.chunks, n.X)),
-            dma((n.chunks,)),
-            dma((n.chunks,)),
+            dma((n.chunks, n.H)),
+            dma((n.chunks, n.H, n.X)),
+            dma((n.chunks, n.H, n.X - 1)),
+            dma((n.chunks, n.H)),
+            dma((n.chunks, n.H)),
+            dma((n.chunks, n.H)),
+            dma((n.W,)),
+            dma((n.W,)),
             dma((2, n.R - 1)),
             dma((2, n.R)),
             dma((2, n.R - 1)),
@@ -551,9 +648,20 @@
             out_specs=(any_,) * 5,
             scratch_shapes=scratch,
             compiler_params=pltpu.CompilerParams(
-                has_side_effects=True, vmem_limit_bytes=60 << 20
+                collective_id=0, has_side_effects=True, vmem_limit_bytes=60 << 20
             ),
-        )(trailing, rows_a, counts_a, factor_a, rows_b, counts_b, factor_b, factor_top, base_a, base_b)
+        )(
+            trailing,
+            rows_a,
+            counts_a,
+            factor_a.reshape(n.slots * PARTS, n.piece, n.width),
+            rows_b,
+            counts_b,
+            factor_b.reshape(n.slots * PARTS, n.piece, n.width),
+            factor_top,
+            base_a,
+            base_b,
+        )
 
     in_specs = (
         P("row", "col"),

time: 148 us -> 121 us (0.82); the launches traced: 146 us -> 121 us
  Pallas kernels: 139 us -> 114 us
    pallas_call x1, Pallas kernels: 139 us -> 114 us  [on_device(): pl.pallas_call(functools.partial(kernel, n), out_shape=(shape(factor_a.sh...]
where the time goes in v2:
time: 121 us
  Pallas kernels  114 us (94%)
  local copies, waits for them, and re-layouts  6 us (5%)
    pallas_call x1, Pallas kernels, on_device(): pl.pallas_call(functools.partial(kernel, n), out_shape=(shape(factor_a.sh...  114 us
    unnamed x13, local copies, waits for them, and re-layouts  6 us

profile of v2, /device:TPU:1, one launch (start us, length us, event | category | flops | bytes accessed | tf_op | source)
XLA Modules:
  0.0 120.8 jit_solution(2185048069956117042)
XLA Ops:
  0.6 114.1 %shard_map.137 = (bf16[1536,512]{1,0:T(8,128)(2,1)}, f32[128,512]{1,0:T(8,128)}, bf16[1536,512]{1,0:T(8,128)(2,1)}, bf16[128,512]{1,0:T(8,128)(2,1)}, f32[128,512]{1,0:T(8,128)}) custom-call(bf16[1536,3072]{1,0:T(8,128)(2,1)} %refs_0_.1, s32[8,12]{1,0:T(8,128)} %refs_1_.1, s32[8]{0:T(128)} %refs_2_.1, bf16[24,64,512]{2,1,0:T(8,128)(2,1)} %bitcast.2, ...), custom_call_target="tpu_custom_call" | custom-call | tf_op jit(solution)/shard_map/pallas_call | solution.py:638
  114.8 0.0 copy-start.2
  114.8 0.0 copy-start
  114.8 2.8 %copy.20 = bf16[1536,512]{1,0:T(8,128)(2,1)} copy(bf16[1536,512]{1,0:T(8,128)(2,1)} %get-tuple-element.10) | data formatting | bytes 3145728
  117.6 0.0 copy-done.2
  117.6 0.7 copy.21
  118.3 0.0 copy-done
  118.3 0.0 copy-start.3
  118.3 0.0 copy-start.1
  118.3 1.1 copy.22
  119.4 0.0 copy-done.3
  119.4 0.7 copy.23
  120.1 0.0 copy-done.1
  120.1 0.7 copy.24
Async XLA Ops:
  114.8 2.8 %copy-start.2 = (f32[128,512]{1,0:T(8,128)S(1)}, f32[128,512]{1,0:T(8,128)}, u32[]{:S(2)}) copy-start(f32[128,512]{1,0:T(8,128)} %get-tuple-element.11) | copy-start | bytes 786436
  114.8 3.5 %copy-start = (bf16[1536,512]{1,0:T(8,128)(2,1)S(1)}, bf16[1536,512]{1,0:T(8,128)(2,1)}, u32[]{:S(2)}) copy-start(bf16[1536,512]{1,0:T(8,128)(2,1)} %get-tuple-element.12) | copy-start | bytes 4718596
  118.3 1.1 copy-start.3
  118.3 1.8 %copy-start.1 = (f32[128,512]{1,0:T(8,128)S(1)}, f32[128,512]{1,0:T(8,128)}, u32[]{:S(2)}) copy-start(f32[128,512]{1,0:T(8,128)} %get-tuple-element.14) | copy-start | bytes 786436

commit v3 on v2

--- a/solution.py
+++ b/solution.py
@@ -10,10 +10,9 @@
 MESH = pl.DeviceIdType.MESH
 LANES = 128
 CORES = 2
-PARTS = 2
+PARTS = 1
 SKEW = 3
-CROSS = 4
-AHEAD = 4
+CROSS = 3
 F32 = jnp.float32
 BF16 = jnp.bfloat16
 
@@ -50,14 +49,15 @@
         self.row_blocks = self.mrows // self.block
         self.X = cols // CORES
         self.Y = self.X
-        while rows % self.Y or self.slots % self.Y:
+        while rows % self.Y:
             self.Y -= 1
         self.Z = rows // self.Y
-        self.sl = self.slots // self.Y
+        self.deep = 2 - self.slots % 2
         self.cw = CORES * LANES
         self.W = self.width // self.cw
         self.chunks = 2 * self.W
-        self.per = self.sl * PARTS
+        self.per = self.slots * PARTS
+        self.Q = self.deep * PARTS
         self.T = self.chunks * self.per
         self.piece = self.block // PARTS
         self.D = SKEW * (self.Z - 1) + CROSS
@@ -84,7 +84,7 @@
         m, fa, fb, ft, ba, bb, held, rhs, acc, own, s1, r1, x2s, x2r, whole_a, whole_b, fin,
         slot_a, slot_b, part_a, part_c, stage, ssend, srecv, agbuf, bsend, brecv, bag,
         diag_a, top, tsend, trecv, tt, diag_b,
-        in_sem, m_sem, src_sem, lane_sem, cross_sem, up_sem, down_sem, y_sem, s1_sem,
+        in_sem, m_sem, src_sem, lane_sem, up_sem, down_sem, y_sem,
         core_s, core_r, xs_sem, xr_sem, xo_s, xo_r, ws_sem, wr_sem, fin_s, fin_r,
         rs_s, rs_r, ag_s, ag_r, t_s, t_r, out_sem,
     ) = refs
@@ -114,13 +114,12 @@
     def source_copies(i):
         for w in range(n.chunks):
             whole = (fa_hbm, fb_hbm)[w // n.W]
-            for j in range(n.Y):
-                for h in range(n.H):
-                    yield pltpu.make_async_copy(
-                        whole.at[pl.ds(j * n.per, n.per), :, pl.ds(n.group(w, h)[0] * LANES, LANES)],
-                        held.at[i, j, pl.ds(w * n.per, n.per), :, pl.ds(h * LANES, LANES)],
-                        src_sem.at[w, j, h],
-                    )
+            for h in range(n.H):
+                yield pltpu.make_async_copy(
+                    whole.at[:, :, pl.ds(n.group(w, h)[0] * LANES, LANES)],
+                    held.at[i, pl.ds(w * n.per, n.per), :, pl.ds(h * LANES, LANES)],
+                    src_sem.at[w, h],
+                )
 
     for i in range(n.fanout):
 
@@ -140,13 +139,6 @@
         )
     ]
 
-    def to_lane(i, u):
-        for dy in range(1, n.Y):
-            to = lax.rem(y + dy, n.Y)
-            other = held.at[i, to, u]
-            dev = (z * n.Y + to, c)
-            remote(other, other, s1_sem.at[dy - 1, i], lane_sem.at[i, u], dev).start()
-
     barrier = pltpu.get_barrier_semaphore()
     peers = [(lax.rem(r + dr, n.R), c) for dr in range(1, n.R)]
     peers += [(r, lax.rem(c + dc, n.C)) for dc in range(1, n.C)]
@@ -159,23 +151,15 @@
         def _():
             for cp in source_copies(i):
                 cp.wait()
-            for u in range(AHEAD):
-                to_lane(i, u)
+
+    trunk = [y == q for q in y0]
 
     def forward(i, t):
         u = t - SKEW * hop[i]
 
-        @pl.when(jnp.logical_and(u >= 0, u < n.T))
+        @pl.when(jnp.logical_and(trunk[i], jnp.logical_and(u >= 0, u < n.T)))
         def _():
-            piece = held.at[i, y, u]
-
-            @pl.when(src[i])
-            def _():
-                later = u + AHEAD
-
-                @pl.when(later < n.T)
-                def _():
-                    to_lane(i, later)
+            piece = held.at[i, u]
 
             @pl.when(jnp.logical_not(src[i]))
             def _():
@@ -190,37 +174,27 @@
                 remote(piece, piece, down_sem.at[i], lane_sem.at[i, u], (r - n.Y, c)).start()
 
             for dy in range(1, n.Y):
-                to = lax.rem(y + dy, n.Y)
-
-                @pl.when(jnp.logical_not(jnp.logical_and(z == z0[i], to == y0[i])))
-                def _():
-                    remote(
-                        piece,
-                        piece,
-                        y_sem.at[dy - 1, i],
-                        cross_sem.at[n.Y - dy - 1, i, u],
-                        (z * n.Y + to, c),
-                    ).start()
+                dev = (z * n.Y + lax.rem(y + dy, n.Y), c)
+                remote(piece, piece, y_sem.at[dy - 1, i], lane_sem.at[i, u], dev).start()
 
     def product(v):
-        s = lax.rem(v, n.sl)
-        first = v < n.W * n.sl
+        s = lax.rem(v, n.slots // n.deep)
+        first = v < n.W * (n.slots // n.deep)
         cols = []
         for i in range(n.fanout):
-            for dy in range(1, n.Y):
-
-                @pl.when(jnp.logical_not(src[i]))
-                def _():
-                    for h in range(PARTS):
-                        u = v * PARTS + h
-                        wait_recv(held.at[i, lax.rem(y + dy, n.Y), u], cross_sem.at[dy - 1, i, u])
+
+            @pl.when(jnp.logical_not(trunk[i]))
+            def _():
+                for h in range(n.Q):
+                    u = v * n.Q + h
+                    wait_recv(held.at[i, u], lane_sem.at[i, u])
 
         for i in range(n.fanout):
             count = jnp.where(first, counts_a[owners[i]], counts_b[owners[i]])
-            for j in range(n.Y):
-                q = j * n.sl + s
+            for j in range(n.deep):
+                q = s * n.deep + j
                 row = jnp.where(first, rows_a[owners[i], q], rows_b[owners[i], q])
-                block = held[i, j, pl.ds(v * PARTS, PARTS)].reshape(B, n.cw)
+                block = held[i, pl.ds(v * n.Q + j * PARTS, PARTS)].reshape(B, n.cw)
                 rhs[len(cols) * B : (len(cols) + 1) * B, :] = kept(block, q, count)
                 cols.append(row * n.fanout + i)
 
@@ -244,9 +218,9 @@
                 forward(i, t)
             late = t - n.D + 1
 
-            @pl.when(jnp.logical_and(late > 0, lax.rem(late, PARTS) == 0))
+            @pl.when(jnp.logical_and(late > 0, lax.rem(late, n.Q) == 0))
             def _():
-                product(lax.div(late, PARTS) - 1)
+                product(lax.div(late, n.Q) - 1)
 
             return carry
 
@@ -463,12 +437,12 @@
     for w in range(last):
         done = (w + 1) * n.per + n.D
         after(done, reduce_core, w)
-        after(done + 1 * PARTS, reduce_x, w)
-        after(done + 4 * PARTS, finish, w)
+        after(done + 1 * n.Q, reduce_x, w)
+        after(done + 4 * n.Q, finish, w)
         if w < last - 1:
-            after(done + 7 * PARTS, relay, w)
-            after(done + 8 * PARTS, gathered, w)
-    after(n.W * n.per + n.D + 8 * PARTS, sums_a)
+            after(done + 7 * n.Q, relay, w)
+            after(done + 8 * n.Q, gathered, w)
+    after(n.W * n.per + n.D + 8 * n.Q, sums_a)
     at = 0
     for t in sorted(set(events) | {n.D, end}):
         if t > at:
@@ -505,26 +479,20 @@
     by_slot(slot_b, whole_b, rows_b, counts_b)
     copy_in(slot_b, col_b_out, out_sem.at[3])
     for i in range(n.fanout):
-        share_of = held.at[i, 0]
-
-        @pl.when(jnp.logical_and(z >= z0[i], z < n.Z - 1))
+        share_of = held.at[i]
+
+        @pl.when(jnp.logical_and(trunk[i], jnp.logical_and(z >= z0[i], z < n.Z - 1)))
         def _():
             wait_recv(share_of, up_sem.at[i])
 
-        @pl.when(jnp.logical_and(z <= z0[i], z > 0))
+        @pl.when(jnp.logical_and(trunk[i], jnp.logical_and(z <= z0[i], z > 0)))
         def _():
             wait_recv(share_of, down_sem.at[i])
 
-        for dy in range(1, n.Y):
-            to = lax.rem(y + dy, n.Y)
-
-            @pl.when(jnp.logical_not(jnp.logical_and(z == z0[i], to == y0[i])))
-            def _():
+        @pl.when(trunk[i])
+        def _():
+            for dy in range(1, n.Y):
                 wait_recv(share_of, y_sem.at[dy - 1, i])
-
-            @pl.when(src[i])
-            def _():
-                wait_recv(share_of, s1_sem.at[dy - 1, i])
 
     for w in range(n.chunks):
         wait_recv(s1.at[w], core_s.at[w])
@@ -562,6 +530,39 @@
         pltpu.make_async_copy(a, b, out_sem.at[j]).wait()
 
 
+def hand_over(*refs):
+    count = (len(refs) - 2) // 3
+    sources, results, held = (refs[j * count : (j + 1) * count] for j in range(3))
+    load_sem, store_sem = refs[-2:]
+    loads = [
+        pltpu.make_async_copy(a, b, load_sem.at[j]) for j, (a, b) in enumerate(zip(sources, held))
+    ]
+    stores = [
+        pltpu.make_async_copy(a, b, store_sem.at[j]) for j, (a, b) in enumerate(zip(held, results))
+    ]
+    for cp in loads:
+        cp.start()
+    for load, store in zip(loads, stores):
+        load.wait()
+        store.start()
+    for cp in stores:
+        cp.wait()
+
+
+def handed_over(arrays):
+    spec = pl.BlockSpec(memory_space=pl.ANY)
+    count = len(arrays)
+    return pl.pallas_call(
+        hand_over,
+        out_shape=tuple(jax.ShapeDtypeStruct(a.shape, a.dtype) for a in arrays),
+        in_specs=[spec] * count,
+        out_specs=(spec,) * count,
+        scratch_shapes=[pltpu.VMEM(a.shape, a.dtype) for a in arrays]
+        + [pltpu.SemaphoreType.DMA((count,))] * 2,
+        compiler_params=pltpu.CompilerParams(vmem_limit_bytes=60 << 20),
+    )(*arrays)
+
+
 def solution(mesh):
     R, C = mesh.shape["row"], mesh.shape["col"]
 
@@ -580,8 +581,8 @@
             vm(factor_top.shape, BF16),
             vm(base_a.shape, F32),
             vm(base_b.shape, F32),
-            vm((n.fanout, n.Y, n.T, n.piece, n.cw), BF16),
-            vm((n.fanout * n.Y * n.block, n.cw), BF16),
+            vm((n.fanout, n.T, n.piece, n.cw), BF16),
+            vm((n.fanout * n.deep * n.block, n.cw), BF16),
             vm((n.mrows, n.cw), F32),
             vm((n.half, n.cw), F32),
             vm((n.chunks, n.half, n.cw), BF16),
@@ -610,12 +611,10 @@
             vm((n.pw, n.width), F32),
             dma((6,)),
             dma((n.mcols // n.block,)),
-            dma((n.chunks, n.Y, n.H)),
+            dma((n.chunks, n.H)),
             dma((n.fanout, n.T)),
-            dma((n.Y - 1, n.fanout, n.T)),
             dma((n.fanout,)),
             dma((n.fanout,)),
-            dma((n.Y - 1, n.fanout)),
             dma((n.Y - 1, n.fanout)),
             dma((n.chunks,)),
             dma((n.chunks,)),
@@ -635,7 +634,7 @@
             dma((n.C,)),
             dma((5,)),
         ]
-        return pl.pallas_call(
+        results = pl.pallas_call(
             functools.partial(kernel, n),
             out_shape=(
                 shape(factor_a.shape, BF16),
@@ -662,6 +661,7 @@
             base_a,
             base_b,
         )
+        return handed_over(results)
 
     in_specs = (
         P("row", "col"),

time: 121 us -> 118 us (0.975)
  local copies, waits for them, and re-layouts: 6 us -> 0 us
  Pallas kernels: 114 us -> 116 us
    unnamed x13 -> x0, local copies, waits for them, and re-layouts: 6 us -> none
    pallas_call x0 -> x1, Pallas kernels: none -> 3.36 us  [handed_over(): pl.pallas_call(hand_over, out_shape=tuple((jax.ShapeDtypeStruct(a.shape,...]
    pallas_call x1, Pallas kernels: 114 us -> 113 us  [on_device(): pl.pallas_call(functools.partial(kernel, n), out_shape=(shape(factor_a.sh...]
where the time goes in v3:
time: 118 us; the launch traced here: 117 us
  Pallas kernels  116 us (98%)
    pallas_call x1, Pallas kernels, on_device(): pl.pallas_call(functools.partial(kernel, n), out_shape=(shape(factor_a.sh...  113 us
    pallas_call x1, Pallas kernels, handed_over(): pl.pallas_call(hand_over, out_shape=tuple((jax.ShapeDtypeStruct(a.shape,...  3.36 us

profile of v3, /device:TPU:1, one launch (start us, length us, event | category | flops | bytes accessed | tf_op | source)
XLA Modules:
  0.0 116.6 jit_solution(10453837590397906126)
XLA Ops:
  0.6 112.6 %shard_map.137 = (bf16[1536,512]{1,0:T(8,128)(2,1)}, f32[128,512]{1,0:T(8,128)}, bf16[1536,512]{1,0:T(8,128)(2,1)}, bf16[128,512]{1,0:T(8,128)(2,1)}, f32[128,512]{1,0:T(8,128)}) custom-call(bf16[1536,3072]{1,0:T(8,128)(2,1)} %refs_0_.1, s32[8,12]{1,0:T(8,128)} %refs_1_.1, s32[8]{0:T(128)} %refs_2_.1, bf16[12,128,512]{2,1,0:T(8,128)(2,1)} %bitcast.2, ...), custom_call_target="tpu_custom_call" | custom-call | tf_op jit(solution)/shard_map/pallas_call | solution.py:637
  113.3 3.4 %shard_map.138 = (bf16[1536,512]{1,0:T(8,128)(2,1)}, f32[128,512]{1,0:T(8,128)}, bf16[1536,512]{1,0:T(8,128)(2,1)}, bf16[128,512]{1,0:T(8,128)(2,1)}, f32[128,512]{1,0:T(8,128)}) custom-call(bf16[1536,512]{1,0:T(8,128)(2,1)} %get-tuple-element.10.refs_0_, f32[128,512]{1,0:T(8,128)} %get-tuple-element.11.refs_1_, ...), custom_call_target="tpu_custom_call" | custom-call | tf_op jit(solution)/shard_map/pallas_call | solution.py:555

commit v4 on v3

--- a/solution.py
+++ b/solution.py
@@ -11,7 +11,7 @@
 LANES = 128
 CORES = 2
 PARTS = 1
-SKEW = 3
+SKEW = 4
 CROSS = 3
 F32 = jnp.float32
 BF16 = jnp.bfloat16
@@ -76,17 +76,20 @@
         g = w % self.W + self.W * h
         return g, g * LANES // (self.pw * CORES)
 
+    def columns(self, g):
+        return [c for c in range(self.C) if c * self.pw // LANES == g]
+
 
 def kernel(n, *refs):
     (
         m_hbm, rows_a, counts_a, fa_hbm, rows_b, counts_b, fb_hbm, ft_hbm, ba_hbm, bb_hbm,
         col_a_out, diag_a_out, col_b_out, top_out, diag_b_out,
-        m, fa, fb, ft, ba, bb, held, rhs, acc, own, s1, r1, x2s, x2r, whole_a, whole_b, fin,
+        m, fa, fb, ft, ba, bb, held, rhs, acc, own, s1, r1, x2s, x2r, whole_a, whole_b, chosen,
         slot_a, slot_b, part_a, part_c, stage, ssend, srecv, agbuf, bsend, brecv, bag,
         diag_a, top, tsend, trecv, tt, diag_b,
         in_sem, m_sem, src_sem, lane_sem, up_sem, down_sem, y_sem,
-        core_s, core_r, xs_sem, xr_sem, xo_s, xo_r, ws_sem, wr_sem, fin_s, fin_r,
-        rs_s, rs_r, ag_s, ag_r, t_s, t_r, out_sem,
+        core_s, core_r, xs_sem, xr_sem, xo_s, xo_r, ws_sem, wr_sem,
+        rs_s, rs_r, bs_s, bs_r, ag_s, ag_r, t_s, t_r, out_sem,
     ) = refs
     B = n.block
     r, c = lax.axis_index("row"), lax.axis_index("col")
@@ -310,13 +313,8 @@
                     total = total + jnp.dot(left, right, preferred_element_type=F32)
                 value = (-total).astype(BF16).reshape(count, B, LANES)
                 wholes[node][g, some] = value
-                if node:
-                    fin[w % n.W, some] = value
 
             half_tiles(f)
-            if node:
-                part = fin.at[w % n.W, mine_blocks]
-                remote(part, part, fin_s.at[w % n.W], fin_r.at[w % n.W], partner).start()
             part = wholes[node].at[g, mine_blocks]
             for dx in range(1, n.X):
                 to = lax.rem(x + dx, n.X)
@@ -324,8 +322,49 @@
                     part, part, xo_s.at[w, h, dx - 1], xo_r.at[w, h], (r, to * CORES + k)
                 ).start()
             to_partner(w, h, g)
+            if node:
+                sums_b(w % n.W, g)
 
         at_owner(w, own_group)
+
+    def to_owners(turn, c_to):
+        kd = c_to % CORES
+        for dr in range(n.R):
+            to = lax.rem(r + dr, n.R)
+            copy = remote(
+                bsend.at[turn, kd, to], brecv.at[r, k], bs_s.at[turn, kd, dr], bs_r.at[r, k], (to, c_to)
+            )
+            yield dr, kd, to, copy
+
+    def sums_b(turn, g):
+        left = whole_b[g, mine_blocks].reshape(n.half, LANES)
+        sums = contract_rows(left, chosen[...])
+        for c_to in n.columns(g):
+            inside = c_to * n.pw - g * LANES
+            kd = c_to % CORES
+            for i in range(n.R):
+                at = inside + i * n.rp
+                bsend[turn, kd, i] = sums[at : at + n.rp].astype(BF16)
+            for dr, kd, to, copy in to_owners(turn, c_to):
+                if dr:
+                    copy.start()
+                else:
+                    pl.when(k != kd)(copy.start)
+
+                    @pl.when(k == kd)
+                    def _():
+                        brecv[r, k] = bsend[turn, kd, to]
+
+    def choose():
+        for cp in loads[:3]:
+            cp.wait()
+        for b in range(n.half_blocks):
+            slot, live = 0, 0
+            for q in range(n.slots):
+                hit = (rows_b[r, q] == k * n.half_blocks + b).astype(jnp.int32)
+                hit = hit * (q < counts_b[r]).astype(jnp.int32)
+                slot, live = slot + q * hit, live + hit
+            chosen[b * B : (b + 1) * B, :] = kept(fb[slot], 0, live)
 
     def relay(w):
         def f(h, g):
@@ -338,14 +377,6 @@
         for h in range(n.H):
             g = n.group(w, h)[0]
             wait_recv(wholes[w // n.W].at[g, other_blocks], wr_sem.at[w, h])
-
-    def fins():
-        for w in range(n.W):
-
-            def f(h, g):
-                wait_recv(fin.at[w, other_blocks], fin_r.at[w])
-
-            at_owner(w, f)
 
     def by_slot(dst, whole, rows, counts):
         for q in range(n.slots):
@@ -370,6 +401,9 @@
         total = recv[0].astype(F32)
         for j in range(1, n.R):
             total = total + recv[j].astype(F32)
+        spread(total, gather_s, gather_r, bag_ref)
+
+    def spread(total, gather_s, gather_r, bag_ref):
         bag_ref[r] = total.astype(BF16)
         for dr in range(1, n.R):
             to = lax.rem(r + dr, n.R)
@@ -380,14 +414,11 @@
             frm = lax.rem(r + dr, n.R)
             wait_recv(bag_ref.at[frm], gather_r.at[frm])
 
-    def end_sends(ref_send, sem_s, bag_ref, gather_s):
+    def end_sends(send, sem_s):
         for dr in range(1, n.R):
-            wait_recv(ref_send.at[0], sem_s.at[dr - 1])
-            wait_recv(bag_ref.at[0], gather_s.at[dr - 1])
+            wait_recv(send.at[0], sem_s.at[dr - 1])
 
     def sums_a():
-        for cp in loads[:3]:
-            cp.wait()
         for q in range(n.slots):
             at = slice(q * B, (q + 1) * B)
             part_a[at, :] = kept(whole_a[group, rows_a[r, q]], q, counts_a[r])
@@ -397,10 +428,10 @@
             mine = stage[pl.ds(inside, n.pw), :]
             for i in range(n.R):
                 ssend[i, j] = mine[i * n.rp : (i + 1) * n.rp].astype(BF16)
-        share(ssend, rs_s.at[0], rs_r.at[0], srecv)
+        share(ssend, rs_s, rs_r, srecv)
 
     def sums_a_add():
-        add_up(srecv, rs_s.at[0], rs_r.at[0], ag_s.at[0], ag_r.at[0], agbuf)
+        add_up(srecv, rs_s, rs_r, ag_s.at[0], ag_r.at[0], agbuf)
 
     def tops():
         gather_sums(agbuf, ag_r.at[0])
@@ -443,6 +474,7 @@
             after(done + 7 * n.Q, relay, w)
             after(done + 8 * n.Q, gathered, w)
     after(n.W * n.per + n.D + 8 * n.Q, sums_a)
+    after(n.W * n.per + n.D + 2 * n.Q, choose)
     at = 0
     for t in sorted(set(events) | {n.D, end}):
         if t > at:
@@ -461,20 +493,14 @@
     by_slot(slot_a, whole_a, rows_a, counts_a)
     copy_in(slot_a, col_a_out, out_sem.at[0])
     finish(last)
-    fins()
-    for q in range(n.slots):
-        part_c[q * B : (q + 1) * B, :] = kept(
-            fin[lax.rem(group, n.W), rows_b[r, q]], q, counts_b[r]
-        )
-    stage[...] = contract_rows(part_c[...], fb[...].reshape(n.N, n.width))
-    mine = stage[pl.ds(inside, n.pw), :]
-    for i in range(n.R):
-        bsend[i] = mine[i * n.rp : (i + 1) * n.rp].astype(BF16)
-    share(bsend, rs_s.at[1], rs_r.at[1], brecv)
+    for dr in range(n.R):
+        frm = lax.rem(r + dr, n.R)
+        for other in (1 - k, k)[: 2 if dr else 1]:
+            wait_recv(brecv.at[frm, other], bs_r.at[frm, other])
+    spread(sum(brecv[j, q].astype(F32) for j in range(n.R) for q in range(CORES)), ag_s.at[1], ag_r.at[1], bag)
+    relay(last)
     tops_in()
     gathered(last - 1)
-    relay(last)
-    add_up(brecv, rs_s.at[1], rs_r.at[1], ag_s.at[1], ag_r.at[1], bag)
     gathered(last)
     by_slot(slot_b, whole_b, rows_b, counts_b)
     copy_in(slot_b, col_b_out, out_sem.at[3])
@@ -500,8 +526,12 @@
         def sent(h, g):
             for dx in range(1, n.X):
                 wait_recv(x2s.at[w, h], xo_s.at[w, h, dx - 1])
-            if w >= n.W:
-                wait_recv(x2s.at[w, h], fin_s.at[w % n.W])
+            for c_to in n.columns(g) if w >= n.W else ():
+                for dr, kd, to, copy in to_owners(w % n.W, c_to):
+                    if dr:
+                        copy.wait_send()
+                    else:
+                        pl.when(k != kd)(copy.wait_send)
 
         def sent_part(h, g):
             wait_recv(x2s.at[w, h], xs_sem.at[w, h])
@@ -516,8 +546,9 @@
     sum_b = jnp.concatenate([bag[i] for i in range(n.R)], axis=0).astype(F32)
     diag_b[...] = bb[...] - sum_b - tt[pl.ds(inside, n.pw), :]
     copy_in(diag_b, diag_b_out, out_sem.at[4])
-    end_sends(ssend, rs_s.at[0], agbuf, ag_s.at[0])
-    end_sends(bsend, rs_s.at[1], bag, ag_s.at[1])
+    end_sends(ssend, rs_s)
+    end_sends(agbuf, ag_s.at[0])
+    end_sends(bag, ag_s.at[1])
     for j, (a, b) in enumerate(
         (
             (slot_a, col_a_out),
@@ -591,7 +622,7 @@
             vm((n.chunks, n.H, n.X, n.half, LANES), BF16),
             vm((n.G,) + blocks, BF16),
             vm((n.G,) + blocks, BF16),
-            vm((n.W,) + blocks, BF16),
+            vm((n.half, n.width), BF16),
             vm(factor_a.shape, BF16),
             vm(factor_b.shape, BF16),
             vm((n.N, LANES), BF16),
@@ -600,8 +631,8 @@
             vm((n.R, 2, n.rp, n.width), BF16),
             vm((n.R, 2, n.rp, n.width), BF16),
             vm((n.R, 2, n.rp, n.width), BF16),
-            vm((n.R, n.rp, n.width), BF16),
-            vm((n.R, n.rp, n.width), BF16),
+            vm((n.W, CORES, n.R, n.rp, n.width), BF16),
+            vm((n.R, CORES, n.rp, n.width), BF16),
             vm((n.R, n.rp, n.width), BF16),
             vm((n.pw, n.width), F32),
             vm((n.pw, n.width), BF16),
@@ -624,10 +655,10 @@
             dma((n.chunks, n.H)),
             dma((n.chunks, n.H)),
             dma((n.chunks, n.H)),
-            dma((n.W,)),
-            dma((n.W,)),
-            dma((2, n.R - 1)),
-            dma((2, n.R)),
+            dma((n.R - 1,)),
+            dma((n.R,)),
+            dma((n.W, CORES, n.R)),
+            dma((n.R, CORES)),
             dma((2, n.R - 1)),
             dma((2, n.R)),
             dma((n.C - 1,)),

time: 118 us -> 116 us (0.983); the launches traced: 117 us -> 116 us
  no operation moved by 1% of the time
where the time goes in v4:
time: 116 us
  Pallas kernels  115 us (99%)
    pallas_call x1, Pallas kernels, on_device(): pl.pallas_call(functools.partial(kernel, n), out_shape=(shape(factor_a.sh...  112 us
    pallas_call x1, Pallas kernels, handed_over(): pl.pallas_call(hand_over, out_shape=tuple((jax.ShapeDtypeStruct(a.shape,...  3.36 us

profile of v4, /device:TPU:1, one launch (start us, length us, event | category | flops | bytes accessed | tf_op | source)
XLA Modules:
  0.0 115.8 jit_solution(7442304733357645858)
XLA Ops:
  0.6 111.8 %shard_map.137 = (bf16[1536,512]{1,0:T(8,128)(2,1)}, f32[128,512]{1,0:T(8,128)}, bf16[1536,512]{1,0:T(8,128)(2,1)}, bf16[128,512]{1,0:T(8,128)(2,1)}, f32[128,512]{1,0:T(8,128)}) custom-call(bf16[1536,3072]{1,0:T(8,128)(2,1)} %refs_0_.1, s32[8,12]{1,0:T(8,128)} %refs_1_.1, s32[8]{0:T(128)} %refs_2_.1, bf16[12,128,512]{2,1,0:T(8,128)(2,1)} %bitcast.2, ...), custom_call_target="tpu_custom_call" | custom-call | tf_op jit(solution)/shard_map/pallas_call | solution.py:668
  112.5 3.4 %shard_map.138 = (bf16[1536,512]{1,0:T(8,128)(2,1)}, f32[128,512]{1,0:T(8,128)}, bf16[1536,512]{1,0:T(8,128)(2,1)}, bf16[128,512]{1,0:T(8,128)(2,1)}, f32[128,512]{1,0:T(8,128)}) custom-call(bf16[1536,512]{1,0:T(8,128)(2,1)} %get-tuple-element.10.refs_0_, f32[128,512]{1,0:T(8,128)} %get-tuple-element.11.refs_1_, ...), custom_call_target="tpu_custom_call" | custom-call | tf_op jit(solution)/shard_map/pallas_call | solution.py:586

commit v5 on v4

--- a/solution.py
+++ b/solution.py
@@ -261,30 +261,37 @@
             theirs = pl.ds(pl.multiple_of((1 - k) * n.half + at, n.htile), n.htile)
             ours = pl.ds(pl.multiple_of(k * n.half + at, n.htile), n.htile)
             s1[w, pl.ds(at, n.htile), :] = acc[theirs, :].astype(BF16)
+            part = s1.at[w, pl.ds(at, n.htile)]
+            step = lax.div(at, n.htile)
+            remote(
+                part, r1.at[w, pl.ds(at, n.htile)], core_s.at[w, step], core_r.at[w, step], partner
+            ).start()
             own[pl.ds(at, n.htile), :] = acc[ours, :]
 
         half_tiles(f)
-        remote(s1.at[w], r1.at[w], core_s.at[w], core_r.at[w], partner).start()
 
     def reduce_x(w):
-        wait_recv(r1.at[w], core_r.at[w])
-
         def f(at):
             rows = pl.ds(at, n.htile)
+            step = lax.div(at, n.htile)
+            wait_recv(r1.at[w, rows], core_r.at[w, step])
             total = own[rows, :] + r1[w, rows, :].astype(F32)
             own[rows, :] = total
             for h in range(n.H):
                 x2s[w, h, rows, :] = total[:, h * LANES : (h + 1) * LANES].astype(BF16)
 
+            def send(h, g):
+                remote(
+                    x2s.at[w, h, rows],
+                    x2r.at[w, h, x, rows],
+                    xs_sem.at[w, h, step],
+                    xr_sem.at[w, h, x, step],
+                    (r, n.group(w, h)[1] * CORES + k),
+                ).start()
+
+            at_owner(w, None, send)
+
         half_tiles(f)
-
-        def send(h, g):
-            chip = n.group(w, h)[1]
-            remote(
-                x2s.at[w, h], x2r.at[w, h, x], xs_sem.at[w, h], xr_sem.at[w, h, x], (r, chip * CORES + k)
-            ).start()
-
-        at_owner(w, None, send)
 
     def to_partner(w, h, g):
         part = wholes[w // n.W].at[g, mine_blocks]
@@ -294,12 +301,11 @@
         node = w // n.W
 
         def own_group(h, g):
-            for dx in range(1, n.X):
-                frm = lax.rem(x + dx, n.X)
-                wait_recv(x2r.at[w, h, frm], xr_sem.at[w, h, frm])
-
             def f(at):
                 rows = pl.ds(at, n.htile)
+                for dx in range(1, n.X):
+                    frm = lax.rem(x + dx, n.X)
+                    wait_recv(x2r.at[w, h, frm, rows], xr_sem.at[w, h, frm, lax.div(at, n.htile)])
                 count = n.htile // B
                 some = pl.ds(k * n.half_blocks + lax.div(at, B), count)
                 total = own[rows, h * LANES : (h + 1) * LANES]
@@ -521,7 +527,8 @@
                 wait_recv(share_of, y_sem.at[dy - 1, i])
 
     for w in range(n.chunks):
-        wait_recv(s1.at[w], core_s.at[w])
+        for step in range(n.half // n.htile):
+            wait_recv(s1.at[w, pl.ds(0, n.htile)], core_s.at[w, step])
 
         def sent(h, g):
             for dx in range(1, n.X):
@@ -534,7 +541,8 @@
                         pl.when(k != kd)(copy.wait_send)
 
         def sent_part(h, g):
-            wait_recv(x2s.at[w, h], xs_sem.at[w, h])
+            for step in range(n.half // n.htile):
+                wait_recv(x2s.at[w, h, pl.ds(0, n.htile)], xs_sem.at[w, h, step])
 
         at_owner(w, sent, sent_part)
         for h in range(n.H):
@@ -647,10 +655,10 @@
             dma((n.fanout,)),
             dma((n.fanout,)),
             dma((n.Y - 1, n.fanout)),
-            dma((n.chunks,)),
-            dma((n.chunks,)),
-            dma((n.chunks, n.H)),
-            dma((n.chunks, n.H, n.X)),
+            dma((n.chunks, n.half // n.htile)),
+            dma((n.chunks, n.half // n.htile)),
+            dma((n.chunks, n.H, n.half // n.htile)),
+            dma((n.chunks, n.H, n.X, n.half // n.htile)),
             dma((n.chunks, n.H, n.X - 1)),
             dma((n.chunks, n.H)),
             dma((n.chunks, n.H)),

time: 116 us -> 116 us (level)
  no operation moved by 1% of the time
where the time goes in v5:
time: 116 us
  Pallas kernels  115 us (99%)
    pallas_call x1, Pallas kernels, on_device(): pl.pallas_call(functools.partial(kernel, n), out_shape=(shape(factor_a.sh...  112 us
    pallas_call x1, Pallas kernels, handed_over(): pl.pallas_call(hand_over, out_shape=tuple((jax.ShapeDtypeStruct(a.shape,...  3.36 us

profile of v5, /device:TPU:1, one launch (start us, length us, event | category | flops | bytes accessed | tf_op | source)
XLA Modules:
  0.0 115.6 jit_solution(7234447717510595567)
XLA Ops:
  0.6 111.6 %shard_map.137 = (bf16[1536,512]{1,0:T(8,128)(2,1)}, f32[128,512]{1,0:T(8,128)}, bf16[1536,512]{1,0:T(8,128)(2,1)}, bf16[128,512]{1,0:T(8,128)(2,1)}, f32[128,512]{1,0:T(8,128)}) custom-call(bf16[1536,3072]{1,0:T(8,128)(2,1)} %refs_0_.1, s32[8,12]{1,0:T(8,128)} %refs_1_.1, s32[8]{0:T(128)} %refs_2_.1, bf16[12,128,512]{2,1,0:T(8,128)(2,1)} %bitcast.2, ...), custom_call_target="tpu_custom_call" | custom-call | tf_op jit(solution)/shard_map/pallas_call | solution.py:676
  112.3 3.4 %shard_map.138 = (bf16[1536,512]{1,0:T(8,128)(2,1)}, f32[128,512]{1,0:T(8,128)}, bf16[1536,512]{1,0:T(8,128)(2,1)}, bf16[128,512]{1,0:T(8,128)(2,1)}, f32[128,512]{1,0:T(8,128)}) custom-call(bf16[1536,512]{1,0:T(8,128)(2,1)} %get-tuple-element.10.refs_0_, f32[128,512]{1,0:T(8,128)} %get-tuple-element.11.refs_1_, ...), custom_call_target="tpu_custom_call" | custom-call | tf_op jit(solution)/shard_map/pallas_call | solution.py:594
